TPU v7x, 32 devices: a whole 2x2x4 slice. The times are simulated.
32 devices in a mesh: wide: 16 (over z, x, core), narrow: 2 (over y).
Axes of the slice: x: 2, y: 2, z: 4, core: 2. Of those that a mesh axis runs over, the one named last changes fastest.
Arguments:
- layer_in: bfloat16 [128, 256, 768], P(('wide', 'narrow')), may hold values from -6 to 6
- segment_ids: int32 [128, 256], P(('wide', 'narrow')), may hold values from 0 to 31, as said below
- live_mask: int32 [128, 256], P(('wide', 'narrow')), may hold values from 0 to 1, as said below
- expert_ids: int32 [128], P(('wide', 'narrow')), may hold values from 1 to 2
- cotangent: bfloat16 [128, 256, 768], P(('wide', 'narrow')), may hold values from -6 to 6
- norm1_gain: float32 [768], replicated, may hold values from 0.1 to 1.9
- norm1_bias: float32 [768], replicated, may hold values from -3 to 3
- q_weight: bfloat16 [768, 768], P('wide'), may hold values from -0.21875 to 0.21875
- q_bias: float32 [768], replicated, may hold values from -3 to 3
- k_weight: bfloat16 [768, 768], P('wide'), may hold values from -0.21875 to 0.21875
- v_weight: bfloat16 [768, 768], P('wide'), may hold values from -0.21875 to 0.21875
- v_bias: float32 [768], replicated, may hold values from -3 to 3
- o_weight: bfloat16 [768, 768], P('wide'), may hold values from -0.875 to 0.875
- o_bias: float32 [768], replicated, may hold values from -3 to 3
- norm2_gain: float32 [768], replicated, may hold values from 0.1 to 1.9
- norm2_bias: float32 [768], replicated, may hold values from -3 to 3
- in_weight: bfloat16 [768, 3072], P('wide'), may hold values from -0.21875 to 0.21875
- in_bias: float32 [3072], replicated, may hold values from -3 to 3
- out_weight: bfloat16 [3072, 768], P('wide'), may hold values from -0.109375 to 0.109375
- out_bias: float32 [768], replicated, may hold values from -3 to 3
Outputs:
- layer_out: bfloat16 [128, 256, 768], P(('wide', 'narrow'))
- input_grad: bfloat16 [128, 256, 768], P(('wide', 'narrow'))
- counts: int32 [3], replicated
- norm1_gain_grad: float32 [768], replicated
- norm1_bias_grad: float32 [768], replicated
- q_weight_grad: float32 [768, 768], P('wide')
- q_bias_grad: float32 [768], replicated
- k_weight_grad: float32 [768, 768], P('wide')
- v_weight_grad: float32 [768, 768], P('wide')
- v_bias_grad: float32 [768], replicated
- o_weight_grad: float32 [768, 768], P('wide')
- o_bias_grad: float32 [768], replicated
- norm2_gain_grad: float32 [768], replicated
- norm2_bias_grad: float32 [768], replicated
- in_weight_grad: float32 [768, 3072], P('wide')
- in_bias_grad: float32 [3072], replicated
- out_weight_grad: float32 [3072, 768], P('wide')
- out_bias_grad: float32 [768], replicated
Inputs may be any that keep to these rules, and one draw needn't show every extreme that they name: `segment_ids`: in each row the captions, 8 to 40 tokens each, lie in order and are numbered from 0; after the last caption the padding slots carry the next number. `live_mask`: the live slots of a row are a prefix of it, at least 8 of them. `expert_ids`: no row names the vision expert.
All inputs are finite; a program needn't handle non-finite values.
Results may differ from a plain program's by a relative error of at most 0.018.
Values may be sent and summed in bfloat16 or wider, within the bound.
A program may use at most 192 MiB of HBM per device.

v0:
```python
import math

import jax
import jax.numpy as jnp
from jax import lax
from jax.sharding import PartitionSpec as P

HEADS = 12


EPSILON = 1e-06
MASKED = -1e30


def norm_rows(values, gain_vec, bias_vec):
    row_mean = jnp.mean(values, axis=-1, keepdims=True)
    centred = values - row_mean
    variance = jnp.mean(centred * centred, axis=-1, keepdims=True)
    return centred * lax.rsqrt(variance + EPSILON) * gain_vec + bias_vec


def gelu_exact(values):
    return jax.nn.gelu(values, approximate=False)


def plain_product(left, right):
    return jnp.dot(left, right, preferred_element_type=jnp.float32)


def product_left_t(left, right):
    return lax.dot_general(
        left, right, (((0,), (0,)), ((), ())), preferred_element_type=jnp.float32
    )


def product_right_t(left, right):
    return lax.dot_general(
        left, right, (((1,), (1,)), ((), ())), preferred_element_type=jnp.float32
    )


def allowed_pairs(seg_rows, live_rows):
    slot_total = seg_rows.shape[-1]
    row_pos = lax.broadcasted_iota(jnp.int32, (slot_total, slot_total), 0)
    col_pos = lax.broadcasted_iota(jnp.int32, (slot_total, slot_total), 1)
    same_seg = seg_rows[:, :, None] == seg_rows[:, None, :]
    return (same_seg & ((live_rows[:, None, :] > 0) | (row_pos == col_pos)[None]))[:, None]


def masked_scores(query_heads, key_heads, seg_rows, live_rows):
    raw_scores = (
        jnp.einsum("gqhe,gkhe->ghqk", query_heads, key_heads, preferred_element_type=jnp.float32)
        * 0.125
    )
    return jnp.where(allowed_pairs(seg_rows, live_rows), raw_scores, MASKED)


def attend_block(pieces):
    query_heads, key_heads, value_heads, seg_rows, live_rows = pieces
    scores = masked_scores(query_heads, key_heads, seg_rows, live_rows)
    row_top = jnp.max(scores, axis=-1, keepdims=True)
    exp_terms = jnp.exp(scores - row_top)
    row_total = jnp.sum(exp_terms, axis=-1, keepdims=True)
    attn_probs = (exp_terms / row_total).astype(jnp.bfloat16)
    mixed_heads = jnp.einsum(
        "ghqk,gkhe->gqhe", attn_probs, value_heads, preferred_element_type=jnp.float32
    )
    return (mixed_heads.astype(jnp.bfloat16), row_top + jnp.log(row_total))


def attend_back(pieces):
    query_heads, key_heads, value_heads, seg_rows, live_rows, log_total, grad_mixed = pieces
    scores = masked_scores(query_heads, key_heads, seg_rows, live_rows)
    attn_probs = jnp.exp(scores - log_total)
    grad_probs = jnp.einsum(
        "gqhe,gkhe->ghqk", grad_mixed, value_heads, preferred_element_type=jnp.float32
    )
    inner_sum = jnp.sum(grad_probs * attn_probs, axis=-1, keepdims=True)
    grad_scores = (attn_probs * (grad_probs - inner_sum)).astype(jnp.bfloat16)
    grad_query = (
        jnp.einsum("ghqk,gkhe->gqhe", grad_scores, key_heads, preferred_element_type=jnp.float32)
        * 0.125
    ).astype(jnp.bfloat16)
    grad_keys = (
        jnp.einsum("ghqk,gqhe->gkhe", grad_scores, query_heads, preferred_element_type=jnp.float32)
        * 0.125
    ).astype(jnp.bfloat16)
    grad_values = jnp.einsum(
        "ghqk,gqhe->gkhe",
        attn_probs.astype(jnp.bfloat16),
        grad_mixed,
        preferred_element_type=jnp.float32,
    ).astype(jnp.bfloat16)
    return (grad_query, grad_keys, grad_values)


def body(
    layer_in,
    segment_ids,
    live_mask,
    expert_ids,
    cotangent,
    norm1_gain,
    norm1_bias,
    q_weight,
    q_bias,
    k_weight,
    v_weight,
    v_bias,
    o_weight,
    o_bias,
    norm2_gain,
    norm2_bias,
    in_weight,
    in_bias,
    out_weight,
    out_bias,
):
    row_local, slot_total, width_all = layer_in.shape
    head_dim = width_all // HEADS
    group_rows = math.gcd(row_local, max(1, 512 // slot_total))
    block_total = row_local // group_rows
    token_total = row_local * slot_total
    live_tokens = jnp.sum(live_mask, axis=1)
    local_counts = jnp.stack(
        [jnp.sum(jnp.where(expert_ids == expert, live_tokens, 0)) for expert in range(3)]
    )
    counts = lax.psum(local_counts, ("wide", "narrow"))
    count_float = counts.astype(jnp.float32)
    own_count = jnp.where(expert_ids == 1, count_float[1], count_float[2])
    row_scale = (count_float[1] + count_float[2]) / (2.0 * own_count)

    def heads_blocks(values):
        return values.reshape(block_total, group_rows, slot_total, HEADS, head_dim)

    seg_blocks = segment_ids.reshape(block_total, group_rows, slot_total)
    live_blocks = live_mask.reshape(block_total, group_rows, slot_total)
    x_rows = layer_in.astype(jnp.float32).reshape(token_total, width_all)
    normed_one = norm_rows(x_rows, norm1_gain, norm1_bias).astype(jnp.bfloat16)
    full_q, full_k, full_v, full_o = (
        lax.all_gather(q_weight, "wide", axis=0, tiled=True),
        lax.all_gather(k_weight, "wide", axis=0, tiled=True),
        lax.all_gather(v_weight, "wide", axis=0, tiled=True),
        lax.all_gather(o_weight, "wide", axis=0, tiled=True),
    )
    query_act = (plain_product(normed_one, full_q) + q_bias).astype(jnp.bfloat16)
    key_act = plain_product(normed_one, full_k).astype(jnp.bfloat16)
    value_act = (plain_product(normed_one, full_v) + v_bias).astype(jnp.bfloat16)
    mixed_blocks, log_total = lax.map(
        attend_block,
        (
            heads_blocks(query_act),
            heads_blocks(key_act),
            heads_blocks(value_act),
            seg_blocks,
            live_blocks,
        ),
    )
    mixed_act = mixed_blocks.reshape(token_total, width_all)
    residual = x_rows + plain_product(mixed_act, full_o) + o_bias
    normed_two = norm_rows(residual, norm2_gain, norm2_bias).astype(jnp.bfloat16)
    full_in, full_out = (
        lax.all_gather(in_weight, "wide", axis=0, tiled=True),
        lax.all_gather(out_weight, "wide", axis=0, tiled=True),
    )
    pre_act = plain_product(normed_two, full_in) + in_bias
    hidden = gelu_exact(pre_act).astype(jnp.bfloat16)
    result = residual + plain_product(hidden, full_out) + out_bias
    layer_out = result.astype(jnp.bfloat16).reshape(row_local, slot_total, width_all)
    token_scale = (live_mask.astype(jnp.float32) * row_scale[:, None]).reshape(token_total, 1)
    grad_y = cotangent.astype(jnp.float32).reshape(token_total, width_all) * token_scale
    grad_branch = grad_y.astype(jnp.bfloat16)
    back_in, back_out = (
        lax.all_gather(in_weight, "wide", axis=0, tiled=True),
        lax.all_gather(out_weight, "wide", axis=0, tiled=True),
    )
    grad_hidden = product_right_t(grad_branch, back_out)
    gelu_pull = jax.vjp(gelu_exact, pre_act)[1]
    grad_pre = gelu_pull(grad_hidden)[0].astype(jnp.bfloat16)
    out_weight_grad = product_left_t(hidden, grad_branch)
    out_bias_grad = jnp.sum(grad_branch.astype(jnp.float32), axis=0)
    in_weight_grad = product_left_t(normed_two, grad_pre)
    in_bias_grad = jnp.sum(grad_pre.astype(jnp.float32), axis=0)
    grad_normed_two = product_right_t(grad_pre, back_in)
    norm_two_pull = jax.vjp(norm_rows, residual, norm2_gain, norm2_bias)[1]
    grad_resid_norm, norm2_gain_grad, norm2_bias_grad = norm_two_pull(grad_normed_two)
    grad_resid = grad_y + grad_resid_norm
    grad_attn = grad_resid.astype(jnp.bfloat16)
    back_q, back_k, back_v, back_o = (
        lax.all_gather(q_weight, "wide", axis=0, tiled=True),
        lax.all_gather(k_weight, "wide", axis=0, tiled=True),
        lax.all_gather(v_weight, "wide", axis=0, tiled=True),
        lax.all_gather(o_weight, "wide", axis=0, tiled=True),
    )
    o_weight_grad = product_left_t(mixed_act, grad_attn)
    o_bias_grad = jnp.sum(grad_attn.astype(jnp.float32), axis=0)
    grad_mixed = product_right_t(grad_attn, back_o).astype(jnp.bfloat16)
    grad_query, grad_keys, grad_values = lax.map(
        attend_back,
        (
            heads_blocks(query_act),
            heads_blocks(key_act),
            heads_blocks(value_act),
            seg_blocks,
            live_blocks,
            log_total,
            heads_blocks(grad_mixed),
        ),
    )
    grad_query = grad_query.reshape(token_total, width_all)
    grad_keys = grad_keys.reshape(token_total, width_all)
    grad_values = grad_values.reshape(token_total, width_all)
    q_weight_grad = product_left_t(normed_one, grad_query)
    q_bias_grad = jnp.sum(grad_query.astype(jnp.float32), axis=0)
    k_weight_grad = product_left_t(normed_one, grad_keys)
    v_weight_grad = product_left_t(normed_one, grad_values)
    v_bias_grad = jnp.sum(grad_values.astype(jnp.float32), axis=0)
    grad_normed_one = (
        product_right_t(grad_query, back_q)
        + product_right_t(grad_keys, back_k)
        + product_right_t(grad_values, back_v)
    )
    norm_one_pull = jax.vjp(norm_rows, x_rows, norm1_gain, norm1_bias)[1]
    grad_x_norm, norm1_gain_grad, norm1_bias_grad = norm_one_pull(grad_normed_one)
    input_grad = (
        (grad_resid + grad_x_norm).astype(jnp.bfloat16).reshape(row_local, slot_total, width_all)
    )
    summed_vectors = lax.psum(
        (
            norm1_gain_grad,
            norm1_bias_grad,
            q_bias_grad,
            v_bias_grad,
            o_bias_grad,
            norm2_gain_grad,
            norm2_bias_grad,
            in_bias_grad,
            out_bias_grad,
        ),
        ("wide", "narrow"),
    )
    row_pieces = (
        lax.psum_scatter(
            q_weight_grad.astype(jnp.bfloat16), "wide", scatter_dimension=0, tiled=True
        ).astype(jnp.float32),
        lax.psum_scatter(
            k_weight_grad.astype(jnp.bfloat16), "wide", scatter_dimension=0, tiled=True
        ).astype(jnp.float32),
        lax.psum_scatter(
            v_weight_grad.astype(jnp.bfloat16), "wide", scatter_dimension=0, tiled=True
        ).astype(jnp.float32),
        lax.psum_scatter(
            o_weight_grad.astype(jnp.bfloat16), "wide", scatter_dimension=0, tiled=True
        ).astype(jnp.float32),
        lax.psum_scatter(
            in_weight_grad.astype(jnp.bfloat16), "wide", scatter_dimension=0, tiled=True
        ).astype(jnp.float32),
        lax.psum_scatter(
            out_weight_grad.astype(jnp.bfloat16), "wide", scatter_dimension=0, tiled=True
        ).astype(jnp.float32),
    )
    row_pieces = (
        lax.psum(row_pieces[0].astype(jnp.bfloat16), "narrow").astype(jnp.float32),
        lax.psum(row_pieces[1].astype(jnp.bfloat16), "narrow").astype(jnp.float32),
        lax.psum(row_pieces[2].astype(jnp.bfloat16), "narrow").astype(jnp.float32),
        lax.psum(row_pieces[3].astype(jnp.bfloat16), "narrow").astype(jnp.float32),
        lax.psum(row_pieces[4].astype(jnp.bfloat16), "narrow").astype(jnp.float32),
        lax.psum(row_pieces[5].astype(jnp.bfloat16), "narrow").astype(jnp.float32),
    )
    return (
        layer_out,
        input_grad,
        counts,
        summed_vectors[0],
        summed_vectors[1],
        row_pieces[0],
        summed_vectors[2],
        row_pieces[1],
        row_pieces[2],
        summed_vectors[3],
        row_pieces[3],
        summed_vectors[4],
        summed_vectors[5],
        summed_vectors[6],
        row_pieces[4],
        summed_vectors[7],
        row_pieces[5],
        summed_vectors[8],
    )


def solution(mesh):
    placed = (
        P(("wide", "narrow"), None, None),
        P(("wide", "narrow"), None),
        P(("wide", "narrow"), None),
        P(("wide", "narrow")),
        P(("wide", "narrow"), None, None),
        P(),
        P(),
        P("wide", None),
        P(),
        P("wide", None),
        P("wide", None),
        P(),
        P("wide", None),
        P(),
        P(),
        P(),
        P("wide", None),
        P(),
        P("wide", None),
        P(),
    )
    return jax.shard_map(
        body,
        mesh=mesh,
        in_specs=placed,
        out_specs=(
            P(("wide", "narrow"), None, None),
            P(("wide", "narrow"), None, None),
            P(),
            P(),
            P(),
            P("wide", None),
            P(),
            P("wide", None),
            P("wide", None),
            P(),
            P("wide", None),
            P(),
            P(),
            P(),
            P("wide", None),
            P(),
            P("wide", None),
            P(),
        ),
        check_vma=False,
    )
```

profile of v0, /device:TPU:0, one launch (start us, length us, event | category | flops | bytes accessed | tf_op | source)
XLA Modules:
  0.0 775.6 jit_solution(13493928599702478998)
XLA Ops:
  18.4 42.4 %psum.112 = s32[3]{0:T(128)S(1)} all-reduce(s32[3]{0:T(128)S(1)} %pad_add_fusion), channel_id=1, replica_groups=mesh['wide'=16,'narrow'=2] {'wide','narrow'}, use_global_device_ids=true, to_apply=%region_12.13 | all-reduce | flops 3 | bytes 24 | tf_op jit(solution)/shard_map/psum | solution.py:128
  68.3 3.8 add_convert_fusion.5
  76.4 14.6 %all-gather.9.cloned.1.call-done = bf16[768,768]{1,0:T(8,128)(2,1)} async-done(((bf16[48,768]{1,0:T(8,128)(2,1)}), bf16[768,768]{1,0:T(8,128)(2,1)}) %all-gather.9.cloned.1.call-update) | async-done | bytes 1179664 | tf_op jit(solution)/shard_map/all_gather | solution.py:141
  98.5 32.1 %all-gather.11.cloned.1.call-done = bf16[768,768]{1,0:T(8,128)(2,1)} async-done(((bf16[48,768]{1,0:T(8,128)(2,1)}), bf16[768,768]{1,0:T(8,128)(2,1)}) %all-gather.11.cloned.1.call-update) | async-done | bytes 1179664 | tf_op jit(solution)/shard_map/all_gather | solution.py:142
  130.6 4.3 convolution_convert_fusion.3
  137.5 3.8 reshape.313
  146.4 16.3 %while.26 = (s32[]{:T(128)}, bf16[2,2,256,12,64]{2,1,0,4,3:T(2,128)(2,1)}, f32[2,2,12,256,1]{3,2,1,4,0:T(8,128)}, bf16[2,2,256,12,64]{2,4,3,1,0:T(8,128)(2,1)}, ...) while((s32[]{:T(128)}, ...), condition=%wide.region_5.6_spmd, body=%wide.region_2.5_spmd.sunk | while | flops 422373888 | bytes 30772356 | solution.py:149
  162.7 3.8 reshape.314
  166.5 3.6 all-gather.13.cloned.1.call-done
  170.1 3.9 fusion.94
  176.2 48.2 %all-gather.15.cloned.1.call-done = bf16[768,3072]{1,0:T(8,128)(2,1)} async-done(((bf16[48,3072]{1,0:T(8,128)(2,1)}), bf16[768,3072]{1,0:T(8,128)(2,1)}) %all-gather.15.cloned.1.call-update) | async-done | bytes 4718608 | tf_op jit(solution)/shard_map/all_gather | solution.py:163
  224.4 38.4 %multiply_convert_fusion.3 = (bf16[1024,3072]{1,0:T(8,128)(2,1)}, f32[1024,3072]{1,0:T(8,128)}, f32[1024,3072]{1,0:T(8,128)}) fusion(f32[3072]{0:T(1024)S(1)} %copy-done.55, bf16[768,3072]{1,0:T(8,128)(2,1)} %all-gather.15.cloned.1.call-done, f32[1024,768]{1,0:T(8,128)} %copy-done.12, f32[768]{0:T(1024)S(1)} %copy-done.59, f32[768]{0:T(1024)S(1)} %copy-done.48, ...), kind=kOutput, calls=%fused_computation.74 | convolution fusion | flops 5043388416 | bytes 39348224 | tf_op jit(solution)/shard_map/dot_general | solution.py:27
  262.8 15.5 %all-gather.17.cloned.1.call-done = bf16[3072,768]{1,0:T(8,128)(2,1)} async-done(((bf16[192,768]{1,0:T(8,128)(2,1)}), bf16[3072,768]{1,0:T(8,128)(2,1)}) %all-gather.17.cloned.1.call-update) | async-done | bytes 4718608 | tf_op jit(solution)/shard_map/all_gather | solution.py:164
  278.4 19.0 %convert_reduce_fusion = (f32[3072]{0:T(1024)}, bf16[1024,3072]{1,0:T(8,128)(2,1)}) fusion(f32[1024,3072]{1,0:T(8,128)} %get-tuple-element.231, bf16[1024,768]{1,0:T(8,128)(2,1)} %fusion.76, bf16[3072,768]{1,0:T(8,128)(2,1)} %all-gather.17.cloned.1.call-done, f32[1024,3072]{1,0:T(8,128)} %get-tuple-element.244, f32[3072]{0:T(1024)S(1)} %copy-done.55), kind=kOutput, calls=%fused_computation.72 | convolution fusion | flops 4885312512 | bytes 37773312 | tf_op jit(solution)/shard_map/dot_general | solution.py:37
  297.4 10.0 %multiply_reduce_fusion.1 = (f32[768]{0:T(1024)}, f32[1024]{0:T(1024)S(1)}, f32[768]{0:T(1024)}, f32[1024,768]{1,0:T(8,128)S(1)}) fusion(f32[1024,768]{1,0:T(8,128)S(1)} %copy-done.13, f32[1024]{0:T(1024)S(1)} %fusion.78, f32[1024]{0:T(1024)S(1)} %broadcast_multiply_fusion, f32[768]{0:T(1024)S(1)} %copy-done.48, ...), kind=kOutput, calls=%fused_computation.115 | convolution fusion | flops 4838126592 | bytes 17323008 | tf_op jit(solution)/shard_map/dot_general | solution.py:37
  314.8 4.0 convolution_convert_fusion.2
  321.4 3.9 reshape.317
  327.5 30.1 %while.27 = (s32[]{:T(128)}, bf16[2,2,256,12,64]{2,4,3,1,0:T(8,128)(2,1)}, bf16[2,2,256,12,64]{2,1,0,4,3:T(2,128)(2,1)}, bf16[2,2,256,12,64]{2,4,3,1,0:T(8,128)(...) while((s32[]{:T(128)}, ...), condition=%wide.region_17.18_spmd, body=%wide.region_15.17_spmd.sunk | while | flops 1032645120 | bytes 109375376 | solution.py:198
  362.2 4.5 convolution_convert_fusion.5
  370.7 4.5 convolution_convert_fusion.7
  377.7 4.5 convolution_convert_fusion.6
  382.3 10.0 %convolution_convert_fusion.1 = bf16[768,3072]{1,0:T(8,128)(2,1)} fusion(bf16[1024,3072]{1,0:T(8,128)(2,1)} %get-tuple-element.248, f32[1024,768]{1,0:T(8,128)S(1)} %copy-done.14, f32[768]{0:T(1024)S(1)} %copy-done.60, f32[768]{0:T(1024)S(1)} %copy-done.48, f32[1024]{0:T(1024)S(1)} %fusion.78, f32[1024]{0:T(1024)S(1)} %broadcast_multiply_fusion), kind=kOutput, calls=%fused_computation.89 | convolution fusion | flops 4838129664 | bytes 14170112 | tf_op jit(solution)/shard_map/dot_general | solution.py:31
  393.7 9.9 %convolution_convert_fusion = bf16[3072,768]{1,0:T(8,128)(2,1)} fusion(bf16[1024,3072]{1,0:T(8,128)(2,1)} %get-tuple-element.230, bf16[1024,768]{1,0:T(8,128)(2,1)S(1)} %copy-done.24), kind=kOutput, calls=%fused_computation.88 | convolution fusion | flops 4834197504 | bytes 12582912 | tf_op jit(solution)/shard_map/dot_general | solution.py:31
  410.7 3.7 fusion.89
  417.6 6.1 add_convert_fusion.2
  423.8 8.5 %reduce-scatter.11.cloned.1.call-done = bf16[48,768]{1,0:T(8,128)(2,1)} async-done(((bf16[768,768]{1,0:T(8,128)(2,1)}), bf16[48,768]{1,0:T(8,128)(2,1)}) %reduce-scatter.11.cloned.1.call-update) | async-done | bytes 73744 | tf_op jit(solution)/shard_map/reduce_scatter | solution.py:249
  432.2 60.7 %reduce-scatter.7.cloned.1.call-done = bf16[48,768]{1,0:T(8,128)(2,1)} async-done(((bf16[768,768]{1,0:T(8,128)(2,1)}), bf16[48,768]{1,0:T(8,128)(2,1)}) %reduce-scatter.7.cloned.1.call-update) | async-done | bytes 73744 | tf_op jit(solution)/shard_map/reduce_scatter | solution.py:243
  493.0 60.6 %reduce-scatter.9.cloned.1.call-done = bf16[48,768]{1,0:T(8,128)(2,1)} async-done(((bf16[768,768]{1,0:T(8,128)(2,1)}), bf16[48,768]{1,0:T(8,128)(2,1)}) %reduce-scatter.9.cloned.1.call-update) | async-done | bytes 73744 | tf_op jit(solution)/shard_map/reduce_scatter | solution.py:246
  553.5 78.5 %reduce-scatter.15.cloned.1.call-done = bf16[48,3072]{1,0:T(8,128)(2,1)} async-done(((bf16[768,3072]{1,0:T(8,128)(2,1)}), bf16[48,3072]{1,0:T(8,128)(2,1)}) %reduce-scatter.15.cloned.1.call-update) | async-done | bytes 294928 | tf_op jit(solution)/shard_map/reduce_scatter | solution.py:255
  632.0 78.8 %reduce-scatter.17.cloned.1.call-done = bf16[192,768]{1,0:T(8,128)(2,1)} async-done(((bf16[3072,768]{1,0:T(8,128)(2,1)}), bf16[192,768]{1,0:T(8,128)(2,1)}) %reduce-scatter.17.cloned.1.call-update) | async-done | bytes 294928 | tf_op jit(solution)/shard_map/reduce_scatter | solution.py:258
  713.3 41.2 %all-reduce = (f32[768]{0:T(1024)}, f32[768]{0:T(1024)}, f32[768]{0:T(1024)}, f32[768]{0:T(1024)}, f32[768]{0:T(1024)}, /*index=5*/f32[768]{0:T(1024)}, f32[768]{0:T(1024)}, f32[3072]{0:T(1024)}, f32[768]{0:T(1024)}) all-reduce(f32[768]{0:T(1024)S(1)} %get-tuple-element.165, ...), channel_id=1, replica_groups=mesh['wide'=16,'narrow'=2] {'wide','narrow'}, use_global_device_ids=true, to_apply=%region_21.22 | all-reduce | flops 9216 | bytes 73728 | tf_op jit(solution)/shard_map/psum | solution.py:228
  754.6 4.5 add_convert_fusion.1
  (293 shorter events, 131.7 us)
Async XLA Ops:
  7.2 56.8 %copy-start.38 = (s32[4,256]{1,0:T(4,128)S(1)}, s32[4,256]{1,0:T(4,128)}, u32[]{:S(2)}) copy-start(s32[4,256]{1,0:T(4,128)} %param.26) | copy-start | bytes 12292
  7.2 8.5 %copy-start.52 = (s32[4]{0:T(128)S(1)}, s32[4]{0:T(128)}, u32[]{:S(2)}) copy-start(s32[4]{0:T(128)} %param.27) | copy-start | bytes 52
  7.2 11.2 %copy-start.49 = (s32[4,256]{1,0:T(4,128)S(1)}, s32[4,256]{1,0:T(4,128)}, u32[]{:S(2)}) copy-start(s32[4,256]{1,0:T(4,128)} %param.25) | copy-start | bytes 12292
  7.2 56.9 %copy-start.32 = (f32[768]{0:T(1024)S(1)}, f32[768]{0:T(1024)}, u32[]{:S(2)}) copy-start(f32[768]{0:T(1024)} %param.29) | copy-start | bytes 9220
  7.2 56.9 %copy-start.44 = (f32[768]{0:T(1024)S(1)}, f32[768]{0:T(1024)}, u32[]{:S(2)}) copy-start(f32[768]{0:T(1024)} %param.30) | copy-start | bytes 9220
  7.3 61.0 %all-gather.7.cloned.1.call-start = ((), (), s32[]{:S(2)}) async-start(), calls=%async_computation.6 | async-start | bytes 1253376 | tf_op jit(solution)/shard_map/all_gather | solution.py:143
  8.0 83.0 %all-gather.9.cloned.1.call-start = ((), (), s32[]{:S(2)}) async-start(), calls=%async_computation.7 | async-start | bytes 1253376 | tf_op jit(solution)/shard_map/all_gather | solution.py:141
  8.7 121.9 %all-gather.11.cloned.1.call-start = ((), (), s32[]{:S(2)}) async-start(), calls=%async_computation.8 | async-start | bytes 1253376 | tf_op jit(solution)/shard_map/all_gather | solution.py:142
  9.5 160.6 %all-gather.13.cloned.1.call-start = ((), (), s32[]{:S(2)}) async-start(), calls=%async_computation.9 | async-start | bytes 1253376 | tf_op jit(solution)/shard_map/all_gather | solution.py:144
  10.1 214.4 %all-gather.15.cloned.1.call-start = ((), (), s32[]{:S(2)}) async-start(), calls=%async_computation.10 | async-start | bytes 5013504 | tf_op jit(solution)/shard_map/all_gather | solution.py:163
  10.6 267.7 %all-gather.17.cloned.1.call-start = ((), (), s32[]{:S(2)}) async-start(), calls=%async_computation.11 | async-start | bytes 5013504 | tf_op jit(solution)/shard_map/all_gather | solution.py:164
  11.2 412.6 %reduce-scatter.13.cloned.1.call-start = ((), (), s32[]{:S(2)}) async-start(), calls=%async_computation.15 | async-start | bytes 1253376 | tf_op jit(solution)/shard_map/reduce_scatter | solution.py:252
  15.7 50.9 %copy-start.36 = (f32[1024]{0:T(1024)}, f32[1024]{0:T(1024)S(1)}, u32[]{:S(2)}) copy-start(f32[1024]{0:T(1024)S(1)} %rsqrt.25) | copy-start | bytes 12292
  15.7 50.9 %copy-start.34 = (f32[1,2,4,128]{3,1,2,0:T(2,128)}, f32[1,2,4,128]{3,1,2,0:T(2,128)S(1)}, u32[]{:S(2)}) copy-start(f32[1,2,4,128]{3,1,2,0:T(2,128)S(1)} %copy.77) | copy-start | bytes 12292
  73.8 17.2 %copy-start.57 = (f32[768]{0:T(1024)S(1)}, f32[768]{0:T(1024)}, u32[]{:S(2)}) copy-start(f32[768]{0:T(1024)} %param.32) | copy-start | bytes 9220
  75.0 16.0 %copy-start.29 = (bf16[1024,768]{1,0:T(8,128)(2,1)S(1)}, bf16[1024,768]{1,0:T(8,128)(2,1)}, u32[]{:S(2)}) copy-start(bf16[1024,768]{1,0:T(8,128)(2,1)} %copy-done.28) | copy-start | bytes 4718596
  162.7 7.4 copy-start.58
  174.0 50.4 %copy-start.48 = (f32[768]{0:T(1024)S(1)}, f32[768]{0:T(1024)}, u32[]{:S(2)}) copy-start(f32[768]{0:T(1024)} %param.38) | copy-start | bytes 9220
  174.0 50.4 %copy-start.55 = (f32[3072]{0:T(1024)S(1)}, f32[3072]{0:T(1024)}, u32[]{:S(2)}) copy-start(f32[3072]{0:T(1024)} %param.41) | copy-start | bytes 36868
  174.0 50.4 %copy-start.59 = (f32[768]{0:T(1024)S(1)}, f32[768]{0:T(1024)}, u32[]{:S(2)}) copy-start(f32[768]{0:T(1024)} %param.39) | copy-start | bytes 9220
  278.4 19.0 %copy-start.13 = (f32[1024,768]{1,0:T(8,128)S(1)}, f32[1024,768]{1,0:T(8,128)}, u32[]{:S(2)}) copy-start(f32[1024,768]{1,0:T(8,128)} %copy-done.12) | copy-start | bytes 9437188
  314.8 117.5 %reduce-scatter.11.cloned.1.call-start = ((), (), s32[]{:S(2)}) async-start(), calls=%async_computation.14 | async-start | bytes 1253376 | tf_op jit(solution)/shard_map/reduce_scatter | solution.py:249
  366.7 126.3 %reduce-scatter.7.cloned.1.call-start = ((), (), s32[]{:S(2)}) async-start(), calls=%async_computation.12 | async-start | bytes 1253376 | tf_op jit(solution)/shard_map/reduce_scatter | solution.py:243
  375.3 178.2 %reduce-scatter.9.cloned.1.call-start = ((), (), s32[]{:S(2)}) async-start(), calls=%async_computation.13 | async-start | bytes 1253376 | tf_op jit(solution)/shard_map/reduce_scatter | solution.py:246
  382.2 249.8 %reduce-scatter.15.cloned.1.call-start = ((), (), s32[]{:S(2)}) async-start(), calls=%async_computation.16 | async-start | bytes 5013504 | tf_op jit(solution)/shard_map/reduce_scatter | solution.py:255
  392.3 318.5 %reduce-scatter.17.cloned.1.call-start = ((), (), s32[]{:S(2)}) async-start(), calls=%async_computation.17 | async-start | bytes 5013504 | tf_op jit(solution)/shard_map/reduce_scatter | solution.py:258
  403.6 355.4 %all-reduce.4.cloned.1.call-start = ((), (), s32[]{:S(2)}) async-start(), calls=%async_computation.18 | async-start | bytes 1769472 | tf_op jit(solution)/shard_map/psum | solution.py:263
  408.5 9.1 %slice-start = ((s8[4718592]{0:T(1024)(128)(4,1)}), s8[4194304]{0:T(1024)(128)(4,1)S(1)}, s32[]{:S(2)}) async-start(s8[4718592]{0:T(1024)(128)(4,1)} %bitcast.232), calls=%async_computation.19 | async-start | bytes 8388608
  408.5 9.1 %slice-start.2 = ((s8[6291456]{0:T(1024)(128)(4,1)}), s8[4194304]{0:T(1024)(128)(4,1)S(1)}, s32[]{:S(2)}) async-start(s8[6291456]{0:T(1024)(128)(4,1)} %bitcast.235), calls=%async_computation.21 | async-start | bytes 8388608
  423.7 289.6 %copy-start.45 = (f32[3072]{0:T(1024)S(1)}, f32[3072]{0:T(1024)}, u32[]{:S(2)}) copy-start(f32[3072]{0:T(1024)} %get-tuple-element.247) | copy-start | bytes 36868
  423.7 289.6 %copy-start.50 = (f32[768]{0:T(1024)S(1)}, f32[768]{0:T(1024)}, u32[]{:S(2)}) copy-start(f32[768]{0:T(1024)} %get-tuple-element.163) | copy-start | bytes 9220
  423.7 289.6 %copy-start.51 = (f32[768]{0:T(1024)S(1)}, f32[768]{0:T(1024)}, u32[]{:S(2)}) copy-start(f32[768]{0:T(1024)} %get-tuple-element.167) | copy-start | bytes 9220
  (58 other events, 158.1 us)
Sparse Core Ops, SparseCore 0:
  10.4 41.0 all-gather.6
  53.7 37.2 all-gather.8
  93.3 37.2 all-gather.10
  132.8 37.2 all-gather.12
  172.2 52.1 all-gather.14
  226.6 51.7 all-gather.16
  314.9 56.6 reduce-scatter.12
  375.1 57.0 reduce-scatter.10
  435.9 57.0 reduce-scatter.6
  496.4 57.0 reduce-scatter.8
  557.4 74.5 reduce-scatter.14
  636.2 74.5 reduce-scatter.16
  713.4 36.9 all-reduce.3
where the time goes:
time: 785 us; the launch traced here: 776 us
  waiting for transfers between devices  405 us (52%)
  matrix products  162 us (21%)
  blocking collectives  83.7 us (11%)
  local copies, waits for them, and re-layouts  65.4 us (8%)
  other arithmetic  42.9 us (5%)
  between operations  16.1 us (2%)
    reduce_scatter x1, waiting for transfers between devices, body(): lax.psum_scatter(out_weight_grad.astype(jnp.bfloat16), 'wide', scatter_di...  78.8 us
    reduce_scatter x1, waiting for transfers between devices, body(): lax.psum_scatter(in_weight_grad.astype(jnp.bfloat16), 'wide', scatter_dim...  78.5 us
    reduce_scatter x1, waiting for transfers between devices, body(): lax.psum_scatter(q_weight_grad.astype(jnp.bfloat16), 'wide', scatter_dime...  60.7 us
    reduce_scatter x1, waiting for transfers between devices, body(): lax.psum_scatter(k_weight_grad.astype(jnp.bfloat16), 'wide', scatter_dime...  60.6 us
    dot_general x6, matrix products, plain_product(): return jnp.dot(left, right, preferred_element_type=jnp.float32)  59.2 us
    all_gather x1, waiting for transfers between devices, body(): lax.all_gather(in_weight, 'wide', axis=0, tiled=True)  48.2 us
    psum x1, blocking collectives, body(): counts = lax.psum(local_counts, ('wide', 'narrow'))  42.4 us
    psum x1, blocking collectives, body(): lax.psum((norm1_gain_grad, norm1_bias_grad, q_bias_grad, v_bias_grad, o_b...  41.2 us
  transfers between devices with their start and end apart: 13, of which 10 were waited for; matrix products, arithmetic and copies ran while one was open for 28% of the time, Pallas kernels for 0%

commit v1 on v0

--- a/solution.py
+++ b/solution.py
@@ -1,11 +1,371 @@
+import functools
 import math
 
 import jax
 import jax.numpy as jnp
 from jax import lax
+from jax.experimental import pallas as pl
+from jax.experimental.pallas import tpu as pltpu
 from jax.sharding import PartitionSpec as P
 
 HEADS = 12
+
+
+MESH = pl.DeviceIdType.MESH
+BF = jnp.bfloat16
+F32 = jnp.float32
+
+
+class Place:
+    def __init__(self, depth, lanes):
+        wide = lax.axis_index("wide")
+        self.depth, self.lanes = depth, lanes
+        self.n = lax.axis_index("narrow")
+        self.c = lax.rem(wide, 2)
+        self.x = lax.rem(wide // 2, 2)
+        self.z = wide // 4
+        self.y = lax.rem(self.n, 2)
+
+    def at(self, z=None, x=None, c=None, n=None):
+        z = self.z if z is None else z
+        x = self.x if x is None else x
+        c = self.c if c is None else c
+        n = self.n if n is None else n
+        return ((z * 2 + x) * 2 + c, n)
+
+    def core(self):
+        return self.at(c=1 - self.c)
+
+    def across_x(self):
+        return self.at(x=1 - self.x)
+
+    def flip_n(self, bit):
+        step = 1 << bit
+        low = lax.rem(self.n // step, 2)
+        return self.n + step * (1 - 2 * low)
+
+    def across_y(self):
+        return self.at(n=self.flip_n(0))
+
+    def along_z(self, step):
+        return self.at(z=lax.rem(self.z + step, self.depth))
+
+    def greet(self):
+        bits = self.lanes.bit_length() - 1
+        others = [self.core(), self.across_x()]
+        others += [self.at(n=self.flip_n(b)) for b in range(bits)]
+        others += [self.along_z(d) for d in range(1, self.depth)]
+        barrier = pltpu.get_barrier_semaphore()
+        for other in others:
+            pl.semaphore_signal(barrier, inc=1, device_id=other, device_id_type=MESH)
+        pl.semaphore_wait(barrier, len(others))
+
+
+class Sems:
+    def __init__(self, send, recv):
+        self.send, self.recv, self.used = send, recv, 0
+        self.open = []
+
+    def copy(self, src, dst, device):
+        i = self.used
+        self.used += 1
+        made = pltpu.make_async_remote_copy(
+            src_ref=src, dst_ref=dst, send_sem=self.send.at[i], recv_sem=self.recv.at[i],
+            device_id=device, device_id_type=MESH,
+        )
+        made.start()
+        self.open.append(made)
+        return made
+
+    def drain(self):
+        for made in self.open:
+            made.wait_send()
+        self.open = []
+
+
+def gather_part(me, sems, view):
+    own = (2 * me.y, 2 * me.y + 1)
+    far = (2 * (1 - me.y), 2 * (1 - me.y) + 1)
+    x, c, z = me.x, me.c, me.z
+    everything = slice(None)
+    hops = []
+    for u in own:
+        hops.append([sems.copy(view(u, z, x, c), view(u, z, x, c), me.along_z(d)) for d in range(1, me.depth)])
+    yield
+    first = []
+    for k, u in enumerate(own):
+        for hop in hops[k]:
+            hop.wait_recv()
+        mine = view(u, everything, x, c)
+        first.append((sems.copy(mine, mine, me.across_x()), sems.copy(mine, mine, me.across_y())))
+        yield
+    (x_a, y_a), (x_b, y_b) = first
+    x_a.wait_recv()
+    there = view(own[0], everything, 1 - x, c)
+    y_fwd = sems.copy(there, there, me.across_y())
+    block = view(own[0], everything, everything, c)
+    cores = [sems.copy(block, block, me.core())]
+    yield
+    y_b.wait_recv()
+    there = view(far[1], everything, x, c)
+    x_fwd = sems.copy(there, there, me.across_x())
+    yield
+    x_b.wait_recv()
+    block = view(own[1], everything, everything, c)
+    cores.append(sems.copy(block, block, me.core()))
+    yield
+    y_a.wait_recv()
+    y_fwd.wait_recv()
+    block = view(far[0], everything, everything, c)
+    cores.append(sems.copy(block, block, me.core()))
+    yield
+    x_fwd.wait_recv()
+    block = view(far[1], everything, everything, c)
+    cores.append(sems.copy(block, block, me.core()))
+    yield
+    for made in cores:
+        made.wait_recv()
+    yield
+
+
+LAG = 2
+SPACE = pltpu.VMEM
+GATHER_COPIES = lambda depth: 2 * (depth - 1) + 4 + 2 + 4
+
+
+def gather_kernel(depth, lanes, halves, q, k, v, o, w_in, w_out, ga, gi, go, local, send, recv):
+    me = Place(depth, lanes)
+    rows, width = q.shape
+    x, c, z = me.x, me.c, me.z
+
+    def fill(pairs):
+        made = [pltpu.make_async_copy(s, d, local.at[i]) for i, (s, d) in enumerate(pairs)]
+        for m in made:
+            m.start()
+        for m in made:
+            m.wait()
+
+    @pl.when(me.y == 0)
+    def _():
+        fill([(q, ga.at[0, z, x, c]), (k, ga.at[1, z, x, c])])
+
+    @pl.when(me.y == 1)
+    def _():
+        fill([(v, ga.at[2, z, x, c]), (o, ga.at[3, z, x, c])])
+
+    pairs = []
+    for kk in range(2):
+        u = 2 * me.y + kk
+        pairs.append((w_in.at[:, pl.ds(pl.multiple_of(u * width, width), width)], gi.at[u, z, x, c]))
+        pairs.append((w_out.at[pl.ds(pl.multiple_of(u * rows, rows), rows), :], go.at[z, x, c, u]))
+    fill(pairs)
+    me.greet()
+    part = width // halves
+    events = []
+    per = GATHER_COPIES(depth)
+    all_sems = []
+    for g in range(3):
+        for h in range(halves):
+            cols = pl.ds(h * part, part)
+
+            def view(u, zs, xs, cs, g=g, cols=cols):
+                if g == 0:
+                    return ga.at[u, zs, xs, cs, :, cols]
+                if g == 1:
+                    return gi.at[u, zs, xs, cs, :, cols]
+                return go.at[zs, xs, cs, u, :, cols]
+
+            i = g * halves + h
+            sems = Sems(send.at[i], recv.at[i])
+            all_sems.append(sems)
+            events.append(gather_part(me, sems, view))
+    order = []
+    for lag in range(64):
+        for i, e in enumerate(events):
+            step = lag - LAG * i
+            if 0 <= step < 10:
+                next(e, None)
+    for s in all_sems:
+        s.drain()
+
+
+def gather_all(depth, lanes, q, k, v, o, w_in, w_out, halves=2):
+    rows, width = q.shape
+    parts = 3 * halves
+    per = GATHER_COPIES(depth)
+    shape = jax.ShapeDtypeStruct((4, depth, 2, 2, rows, width), BF)
+    shape_o = jax.ShapeDtypeStruct((depth, 2, 2, 4, rows, width), BF)
+    anyspec = pl.BlockSpec(memory_space=pl.ANY); vspec = pl.BlockSpec(memory_space=SPACE)
+    return pl.pallas_call(
+        functools.partial(gather_kernel, depth, lanes, halves),
+        out_shape=(shape, shape, shape_o),
+        in_specs=[anyspec] * 6,
+        out_specs=(vspec,) * 3,
+        scratch_shapes=[
+            pltpu.SemaphoreType.DMA((4,)),
+            pltpu.SemaphoreType.DMA((parts, per)),
+            pltpu.SemaphoreType.DMA((parts, per)),
+        ],
+        compiler_params=pltpu.CompilerParams(collective_id=0, has_side_effects=True, vmem_limit_bytes=60 << 20),
+        name="gather_all",
+    )(q, k, v, o, w_in, w_out)
+
+
+def reduce_part(me, sems, view, far_view, bufs, emit):
+    rc, ry, rx, rz, fin, far = bufs
+    a, b = 2 * me.y, 2 * me.y + 1
+    ta, tb = 2 * (1 - me.y), 2 * (1 - me.y) + 1
+    x, c, z = me.x, me.c, me.z
+    every = slice(None)
+    bits = me.lanes.bit_length() - 1
+
+    def add(dst, *terms):
+        total = dst[...].astype(F32)
+        for t in terms:
+            total = total + t[...].astype(F32)
+        dst[...] = total.astype(BF)
+
+    cores = {}
+    for i, u in enumerate((ta, tb, b, a)):
+        cores[i] = sems.copy(view(u, every, every, 1 - c), rc.at[i], me.core())
+    yield
+    cores[0].wait_recv()
+    add(view(ta, every, every, c), rc.at[0])
+    y_diag = sems.copy(view(ta, every, 1 - x, c), ry.at[0], me.across_y())
+    yield
+    cores[1].wait_recv()
+    add(view(tb, every, every, c), rc.at[1])
+    x_diag = sems.copy(view(tb, every, 1 - x, c), rx.at[0], me.across_x())
+    yield
+    cores[2].wait_recv()
+    add(view(b, every, every, c), rc.at[2])
+    x_near = sems.copy(view(b, every, 1 - x, c), rx.at[1], me.across_x())
+    y_near = sems.copy(view(ta, every, x, c), ry.at[1], me.across_y())
+    cores[3].wait_recv()
+    add(view(a, every, every, c), rc.at[3])
+    yield
+    y_diag.wait_recv()
+    add(view(a, every, 1 - x, c), ry.at[0])
+    x_last = sems.copy(view(a, every, 1 - x, c), rx.at[2], me.across_x())
+    yield
+    x_diag.wait_recv()
+    add(view(tb, every, x, c), rx.at[0])
+    y_last = sems.copy(view(tb, every, x, c), ry.at[2], me.across_y())
+    yield
+    y_near.wait_recv()
+    x_last.wait_recv()
+    add(view(a, every, x, c), ry.at[1], rx.at[2])
+    z_hops = []
+    hop = []
+    for d in range(1, me.depth):
+        to = lax.rem(z + d, me.depth)
+        hop.append(sems.copy(view(a, to, x, c), rz.at[0, d - 1], me.along_z(d)))
+    z_hops.append(hop)
+    yield
+    x_near.wait_recv()
+    y_last.wait_recv()
+    add(view(b, every, x, c), rx.at[1], ry.at[2])
+    hop = []
+    for d in range(1, me.depth):
+        to = lax.rem(z + d, me.depth)
+        hop.append(sems.copy(view(b, to, x, c), rz.at[1, d - 1], me.along_z(d)))
+    z_hops.append(hop)
+    yield
+    sent = []
+    for k, u in enumerate((a, b)):
+        for h in z_hops[k]:
+            h.wait_recv()
+        total = view(u, z, x, c)[...].astype(F32)
+        for d in range(1, me.depth):
+            total = total + rz[k, d - 1].astype(F32)
+        fin[0, k] = total.astype(BF)
+        for bit in range(1, bits):
+            swap = sems.copy(fin.at[bit - 1, k], far.at[bit, k], me.at(n=me.flip_n(bit)))
+            swap.wait_recv()
+            total = fin[bit - 1, k].astype(F32) + far[bit, k].astype(F32)
+            fin[bit, k] = total.astype(BF)
+        last = max(bits - 1, 0)
+        sent.append(sems.copy(fin.at[last, k], far.at[0, k], me.across_y()))
+        emit(u, fin[last, k])
+        yield
+    for k, u in enumerate((ta, tb)):
+        sent[k].wait_recv()
+        emit(u, far[0, k])
+        yield
+
+
+def reduce_copies(depth, lanes):
+    bits = lanes.bit_length() - 1
+    return 4 + 6 + 2 * (depth - 1) + 2 * (bits - 1) + 2
+
+
+REDUCE_STEPS = 12
+
+
+def reduce_kernel(depth, lanes, halves, ga, gi, go, ra, ri, ro, wa, wi, wo, rc, ry, rx, rz, fin, far, local, send, recv):
+    me = Place(depth, lanes)
+    loads = [pltpu.make_async_copy(s, d, local.at[i]) for i, (s, d) in enumerate(((ga, wa), (gi, wi), (go, wo)))]
+    for m in loads:
+        m.start()
+    me.greet()
+    for m in loads:
+        m.wait()
+    width = wa.shape[-1]
+    part = width // halves
+    events, all_sems = [], []
+    for g in range(3):
+        for h in range(halves):
+            cols = pl.ds(h * part, part)
+            i = g * halves + h
+
+            def view(u, zs, xs, cs, g=g, cols=cols):
+                if g == 0:
+                    return wa.at[u, zs, xs, cs, :, cols]
+                if g == 1:
+                    return wi.at[u, zs, xs, cs, :, cols]
+                return wo.at[zs, xs, cs, u, :, cols]
+
+            def emit(u, value, g=g, cols=cols):
+                (ra, ri, ro)[g][u, :, cols] = value.astype(F32)
+
+            sems = Sems(send.at[i], recv.at[i])
+            all_sems.append(sems)
+            bufs = [t.at[i] for t in (rc, ry, rx, rz, fin, far)]
+            events.append(reduce_part(me, sems, view, None, bufs, emit))
+    for lag in range(100):
+        for i, e in enumerate(events):
+            step = lag - LAG * i
+            if 0 <= step < REDUCE_STEPS + 1:
+                next(e, None)
+    for s in all_sems:
+        s.drain()
+
+
+def reduce_all(depth, lanes, ga, gi, go, halves=2):
+    rows, width = ga.shape[-2:]
+    parts, part = 3 * halves, width // halves
+    per = reduce_copies(depth, lanes)
+    bits = lanes.bit_length() - 1
+    anyspec = pl.BlockSpec(memory_space=pl.ANY)
+    vspec = pl.BlockSpec(memory_space=pltpu.VMEM)
+    out = jax.ShapeDtypeStruct((4, rows, width), F32)
+    v = lambda *s: pltpu.VMEM(s, BF)
+    return pl.pallas_call(
+        functools.partial(reduce_kernel, depth, lanes, halves),
+        out_shape=(out, out, out),
+        in_specs=[anyspec] * 3,
+        out_specs=(vspec,) * 3,
+        scratch_shapes=[
+            v(*ga.shape), v(*gi.shape), v(*go.shape),
+            v(parts, 4, depth, 2, rows, part), v(parts, 3, depth, rows, part), v(parts, 3, depth, rows, part),
+            v(parts, 2, depth - 1, rows, part), v(parts, max(bits, 1), 2, rows, part), v(parts, max(bits, 1), 2, rows, part),
+            pltpu.SemaphoreType.DMA((3,)),
+            pltpu.SemaphoreType.DMA((parts, per)),
+            pltpu.SemaphoreType.DMA((parts, per)),
+        ],
+        compiler_params=pltpu.CompilerParams(collective_id=1, has_side_effects=True, vmem_limit_bytes=60 << 20),
+        name="reduce_all",
+    )(ga, gi, go)
 
 
 EPSILON = 1e-06
@@ -137,12 +497,16 @@
     live_blocks = live_mask.reshape(block_total, group_rows, slot_total)
     x_rows = layer_in.astype(jnp.float32).reshape(token_total, width_all)
     normed_one = norm_rows(x_rows, norm1_gain, norm1_bias).astype(jnp.bfloat16)
+    wide_total, narrow_total = lax.axis_size("wide"), lax.axis_size("narrow")
+    depth = wide_total // 4
+    got_a, got_i, got_o = gather_all(
+        depth, narrow_total, q_weight, k_weight, v_weight, o_weight, in_weight, out_weight
+    )
     full_q, full_k, full_v, full_o = (
-        lax.all_gather(q_weight, "wide", axis=0, tiled=True),
-        lax.all_gather(k_weight, "wide", axis=0, tiled=True),
-        lax.all_gather(v_weight, "wide", axis=0, tiled=True),
-        lax.all_gather(o_weight, "wide", axis=0, tiled=True),
-    )
+        got_a[i].reshape(width_all, width_all) for i in range(4)
+    )
+    full_in = got_i.reshape(4, width_all, width_all).transpose(1, 0, 2).reshape(width_all, -1)
+    full_out = got_o.reshape(-1, width_all)
     query_act = (plain_product(normed_one, full_q) + q_bias).astype(jnp.bfloat16)
     key_act = plain_product(normed_one, full_k).astype(jnp.bfloat16)
     value_act = (plain_product(normed_one, full_v) + v_bias).astype(jnp.bfloat16)
@@ -159,10 +523,6 @@
     mixed_act = mixed_blocks.reshape(token_total, width_all)
     residual = x_rows + plain_product(mixed_act, full_o) + o_bias
     normed_two = norm_rows(residual, norm2_gain, norm2_bias).astype(jnp.bfloat16)
-    full_in, full_out = (
-        lax.all_gather(in_weight, "wide", axis=0, tiled=True),
-        lax.all_gather(out_weight, "wide", axis=0, tiled=True),
-    )
     pre_act = plain_product(normed_two, full_in) + in_bias
     hidden = gelu_exact(pre_act).astype(jnp.bfloat16)
     result = residual + plain_product(hidden, full_out) + out_bias
@@ -170,10 +530,7 @@
     token_scale = (live_mask.astype(jnp.float32) * row_scale[:, None]).reshape(token_total, 1)
     grad_y = cotangent.astype(jnp.float32).reshape(token_total, width_all) * token_scale
     grad_branch = grad_y.astype(jnp.bfloat16)
-    back_in, back_out = (
-        lax.all_gather(in_weight, "wide", axis=0, tiled=True),
-        lax.all_gather(out_weight, "wide", axis=0, tiled=True),
-    )
+    back_in, back_out = full_in, full_out
     grad_hidden = product_right_t(grad_branch, back_out)
     gelu_pull = jax.vjp(gelu_exact, pre_act)[1]
     grad_pre = gelu_pull(grad_hidden)[0].astype(jnp.bfloat16)
@@ -186,12 +543,7 @@
     grad_resid_norm, norm2_gain_grad, norm2_bias_grad = norm_two_pull(grad_normed_two)
     grad_resid = grad_y + grad_resid_norm
     grad_attn = grad_resid.astype(jnp.bfloat16)
-    back_q, back_k, back_v, back_o = (
-        lax.all_gather(q_weight, "wide", axis=0, tiled=True),
-        lax.all_gather(k_weight, "wide", axis=0, tiled=True),
-        lax.all_gather(v_weight, "wide", axis=0, tiled=True),
-        lax.all_gather(o_weight, "wide", axis=0, tiled=True),
-    )
+    back_q, back_k, back_v, back_o = full_q, full_k, full_v, full_o
     o_weight_grad = product_left_t(mixed_act, grad_attn)
     o_bias_grad = jnp.sum(grad_attn.astype(jnp.float32), axis=0)
     grad_mixed = product_right_t(grad_attn, back_o).astype(jnp.bfloat16)
@@ -239,33 +591,27 @@
         ),
         ("wide", "narrow"),
     )
+    rows = width_all // wide_total
+    low = lambda t: t.astype(jnp.bfloat16)
+    split = (depth, 2, 2)
+    term_a = jnp.stack(
+        [low(t) for t in (q_weight_grad, k_weight_grad, v_weight_grad, o_weight_grad)]
+    ).reshape(4, *split, rows, width_all)
+    term_i = (
+        low(in_weight_grad)
+        .reshape(width_all, 4, width_all)
+        .transpose(1, 0, 2)
+        .reshape(4, *split, rows, width_all)
+    )
+    term_o = low(out_weight_grad).reshape(*split, 4, rows, width_all)
+    sum_a, sum_i, sum_o = reduce_all(depth, narrow_total, term_a, term_i, term_o)
     row_pieces = (
-        lax.psum_scatter(
-            q_weight_grad.astype(jnp.bfloat16), "wide", scatter_dimension=0, tiled=True
-        ).astype(jnp.float32),
-        lax.psum_scatter(
-            k_weight_grad.astype(jnp.bfloat16), "wide", scatter_dimension=0, tiled=True
-        ).astype(jnp.float32),
-        lax.psum_scatter(
-            v_weight_grad.astype(jnp.bfloat16), "wide", scatter_dimension=0, tiled=True
-        ).astype(jnp.float32),
-        lax.psum_scatter(
-            o_weight_grad.astype(jnp.bfloat16), "wide", scatter_dimension=0, tiled=True
-        ).astype(jnp.float32),
-        lax.psum_scatter(
-            in_weight_grad.astype(jnp.bfloat16), "wide", scatter_dimension=0, tiled=True
-        ).astype(jnp.float32),
-        lax.psum_scatter(
-            out_weight_grad.astype(jnp.bfloat16), "wide", scatter_dimension=0, tiled=True
-        ).astype(jnp.float32),
-    )
-    row_pieces = (
-        lax.psum(row_pieces[0].astype(jnp.bfloat16), "narrow").astype(jnp.float32),
-        lax.psum(row_pieces[1].astype(jnp.bfloat16), "narrow").astype(jnp.float32),
-        lax.psum(row_pieces[2].astype(jnp.bfloat16), "narrow").astype(jnp.float32),
-        lax.psum(row_pieces[3].astype(jnp.bfloat16), "narrow").astype(jnp.float32),
-        lax.psum(row_pieces[4].astype(jnp.bfloat16), "narrow").astype(jnp.float32),
-        lax.psum(row_pieces[5].astype(jnp.bfloat16), "narrow").astype(jnp.float32),
+        sum_a[0],
+        sum_a[1],
+        sum_a[2],
+        sum_a[3],
+        sum_i.transpose(1, 0, 2).reshape(rows, -1),
+        sum_o.reshape(4 * rows, width_all),
     )
     return (
         layer_out,

time: 785 us -> 498 us (0.63)
  waiting for transfers between devices: 405 us -> 0 us
  Pallas kernels: 0 us -> 162 us
  matrix products: 162 us -> 141 us
  between operations: 16.1 us -> 2.96 us
  other arithmetic: 42.9 us -> 29.8 us
  local copies, waits for them, and re-layouts: 65.4 us -> 75.7 us
    reduce_scatter x6 -> x0, waiting for transfers between devices: 287 us -> none  [the longest x1 78.8 us: body(): lax.psum_scatter(out_weight_grad.astype(jnp.bfloat16), 'wide', scatter_di...]
    pallas_call x0 -> x2, Pallas kernels: none -> 162 us  [the longest x1 81.1 us: gather_all(): pl.pallas_call(functools.partial(gather_kernel, depth, lanes, halves), ou...]
    all_gather x6 -> x0, waiting for transfers between devices: 114 us -> none  [the longest x1 48.2 us: body(): lax.all_gather(in_weight, 'wide', axis=0, tiled=True)]
    dot_general x6, matrix products: 35.8 us -> 19.2 us  [product_left_t(): lax.dot_general(left, right, (((0,), (0,)), ((), ())), preferred_element_...]
    convert_element_type x7 -> x0, other arithmetic: 14.4 us -> none  [the longest x1 4.51 us: body(): (grad_resid + grad_x_norm).astype(jnp.bfloat16)]
    reshape x0 -> x3, local copies, waits for them, and re-layouts: none -> 11.2 us  [the longest x1 6.66 us: body(): got_i.reshape(4, width_all, width_all).transpose(1, 0, 2)]
  transfers between devices with their start and end apart: 13 -> 0, of which waited for: 10 -> 0; matrix products, arithmetic and copies ran while one was open for 28% -> 0% of each run, Pallas kernels for 0% -> 0%
where the time goes in v1:
time: 498 us; the launch traced here: 494 us
  Pallas kernels  162 us (33%)
  matrix products  141 us (28%)
  blocking collectives  81.7 us (16%)
  local copies, waits for them, and re-layouts  75.7 us (15%)
  other arithmetic  29.8 us (6%)
    pallas_call x1, Pallas kernels, gather_all(): pl.pallas_call(functools.partial(gather_kernel, depth, lanes, halves), ou...  81.1 us
    pallas_call x1, Pallas kernels, reduce_all(): pl.pallas_call(functools.partial(reduce_kernel, depth, lanes, halves), ou...  80.9 us
    dot_general x6, matrix products, plain_product(): return jnp.dot(left, right, preferred_element_type=jnp.float32)  55.6 us
    dot_general x6, matrix products, product_right_t(): lax.dot_general(left, right, (((1,), (1,)), ((), ())), preferred_element_...  42.7 us
    psum x1, blocking collectives, body(): lax.psum((norm1_gain_grad, norm1_bias_grad, q_bias_grad, v_bias_grad, o_b...  41.9 us
    psum x1, blocking collectives, body(): counts = lax.psum(local_counts, ('wide', 'narrow'))  39.8 us
    dot_general x6, matrix products, product_left_t(): lax.dot_general(left, right, (((0,), (0,)), ((), ())), preferred_element_...  19.2 us

profile of v1, /device:TPU:0, one launch (start us, length us, event | category | flops | bytes accessed | tf_op | source)
XLA Modules:
  0.0 493.6 jit_solution(8845419015623118074)
XLA Ops:
  6.3 81.1 %gather_all.1 = (bf16[4,4,2,2,48,768]{5,4,3,2,1,0:T(8,128)(2,1)}, bf16[4,4,2,2,48,768]{5,4,3,2,1,0:T(8,128)(2,1)}, bf16[4,2,2,4,48,768]{5,4,3,2,1,0:T(8,128)(2,1)}) custom-call(bf16[48,768]{1,0:T(8,128)(2,1)} %q.1, bf16[48,768]{1,0:T(8,128)(2,1)} %k.1, bf16[48,768]{1,0:T(8,128)(2,1)} %v.1, bf16[48,768]{1,0:T(8,128)(2,1)} %o.1, bf16[48,3072]{1,0:T(8,128)(2,1)} %w_in.1, ...), custom_call_target="tpu_custom_call" | custom-call | tf_op jit(solution)/shard_map/gather_all/pallas_call | solution.py:199
  87.5 4.2 fusion.90
  103.8 2.5 convolution_convert_fusion.3
  108.1 2.4 reshape.411
  114.4 12.6 %while.26 = (s32[]{:T(128)}, bf16[2,2,256,12,64]{2,1,0,4,3:T(2,128)(2,1)}, f32[2,2,12,256,1]{3,2,1,4,0:T(8,128)S(1)}, bf16[2,2,256,12,64]{2,4,3,1,0:T(8,128)(2,1...) while((s32[]{:T(128)}, ...), condition=%wide.region_5.6_spmd, body=%wide.region_2.5_spmd.sunk | while | flops 422373888 | bytes 30788232 | solution.py:513
  127.1 4.8 reshape.412
  131.9 3.9 fusion.92
  137.5 6.7 %copy.61 = bf16[4,768,768]{1,2,0:T(8,128)(2,1)} copy(bf16[4,768,768]{2,1,0:T(8,128)(2,1)} %bitcast.251) | data formatting | bytes 9437184 | tf_op jit(solution)/shard_map/reshape | solution.py:508
  144.2 36.9 %multiply_convert_fusion.3 = (bf16[1024,3072]{1,0:T(8,128)(2,1)}, f32[1024,3072]{1,0:T(8,128)}, f32[1024,3072]{1,0:T(8,128)}) fusion(f32[3072]{0:T(1024)S(1)} %copy-done.62, bf16[768,3072]{0,1:T(8,128)(2,1)} %bitcast.252, f32[1024,768]{1,0:T(8,128)} %copy-done.15, f32[768]{0:T(1024)S(1)} %copy-done.66, f32[768]{0:T(1024)S(1)} %copy-done.57, ...), kind=kOutput, calls=%fused_computation.74 | convolution fusion | flops 5043388416 | bytes 39348224 | tf_op jit(solution)/shard_map/dot_general | solution.py:387
  183.9 39.8 %psum.70 = s32[3]{0:T(128)S(1)} all-reduce(s32[3]{0:T(128)S(1)} %pad_add_fusion), channel_id=1, replica_groups=mesh['wide'=16,'narrow'=2] {'wide','narrow'}, use_global_device_ids=true, to_apply=%region_12.13 | all-reduce | flops 3 | bytes 24 | tf_op jit(solution)/shard_map/psum | solution.py:488
  228.0 17.6 %convert_reduce_fusion = (f32[3072]{0:T(1024)}, bf16[1024,3072]{1,0:T(8,128)(2,1)}) fusion(f32[1024,3072]{1,0:T(8,128)} %get-tuple-element.239, bf16[1024,768]{1,0:T(8,128)(2,1)S(1)} %bitcast.262, bf16[3072,768]{1,0:T(8,128)(2,1)} %bitcast.282, f32[1024,3072]{1,0:T(8,128)} %get-tuple-element.264, f32[3072]{0:T(1024)S(1)} %copy-done.62), kind=kOutput, calls=%fused_computation.72 | convolution fusion | flops 4885312512 | bytes 37773312 | tf_op jit(solution)/shard_map/dot_general | solution.py:397
  245.5 9.7 %multiply_reduce_fusion.1 = (f32[768]{0:T(1024)}, f32[1024]{0:T(1024)S(1)}, f32[768]{0:T(1024)}, f32[1024,768]{1,0:T(8,128)S(1)}) fusion(f32[1024,768]{1,0:T(8,128)S(1)} %copy-done.16, f32[1024]{0:T(1024)S(1)} %fusion.75, f32[1024]{0:T(1024)S(1)} %broadcast_multiply_fusion, f32[768]{0:T(1024)S(1)} %copy-done.57, ...), kind=kOutput, calls=%fused_computation.113 | convolution fusion | flops 4838126592 | bytes 17323008 | tf_op jit(solution)/shard_map/dot_general | solution.py:397
  262.6 4.0 reshape.418
  268.8 28.8 %while.27 = (s32[]{:T(128)}, bf16[2,2,256,12,64]{2,4,3,1,0:T(8,128)(2,1)}, bf16[2,2,256,12,64]{2,1,0,4,3:T(2,128)(2,1)}, bf16[2,2,256,12,64]{2,4,3,1,0:T(8,128)(...) while((s32[]{:T(128)}, ...), condition=%wide.region_17.18_spmd, body=%wide.region_15.17_spmd.sunk | while | flops 1032645120 | bytes 109375376 | solution.py:550
  269.3 2.3 fusion.159
  280.9 2.5 fusion.163
  283.6 2.3 fusion.159
  295.2 2.5 fusion.163
  297.6 3.3 reshape.420
  301.0 3.1 fusion.94
  306.9 5.0 %fusion.93 = f32[1024,768]{1,0:T(8,128)} fusion(bf16[1024,768]{0,1:T(8,128)(2,1)S(1)} %reshape.419, bf16[768,768]{1,0:T(8,128)(2,1)} %bitcast.263), kind=kOutput, calls=%fused_computation.169 | convolution fusion | flops 1207959552 | bytes 5898240 | tf_op jit(solution)/shard_map/dot_general | solution.py:397
  311.8 3.1 copy.69
  315.0 2.3 reshape.421
  317.4 5.9 %fusion.86 = (f32[768]{0:T(1024)S(1)}, f32[1024]{0:T(1024)S(1)}, f32[1024,768]{1,0:T(8,128)S(1)}) fusion(f32[768]{0:T(1024)S(1)} %copy-done.49, f32[1024]{0:T(1024)S(1)} %bitcast.276, bf16[4,256,768]{2,1,0:T(8,128)(2,1)S(1)} %copy-done.7, bf16[1024,768]{0,1:T(8,128)(2,1)} %reshape.421, bf16[768,768]{1,0:T(8,128)(2,1)} %bitcast.250, ...), kind=kOutput, calls=%fused_computation.164 | convolution fusion | flops 1214249216 | bytes 13776896 | tf_op jit(solution)/shard_map/dot_general | solution.py:397
  325.7 2.6 fusion.73
  328.3 7.1 %convolution_convert_fusion = bf16[3072,768]{1,0:T(8,128)(2,1)} fusion(bf16[1024,3072]{1,0:T(8,128)(2,1)S(1)} %bitcast.288, bf16[1024,768]{1,0:T(8,128)(2,1)S(1)} %get-tuple-element.248), kind=kOutput, calls=%fused_computation.88 | convolution fusion | flops 4834197504 | bytes 12582912 | tf_op jit(solution)/shard_map/dot_general | solution.py:391
  335.4 6.4 %convolution_convert_fusion.1 = bf16[768,3072]{1,0:T(8,128)(2,1)S(1)} fusion(bf16[1024,3072]{1,0:T(8,128)(2,1)S(1)} %bitcast.286, f32[1024,768]{1,0:T(8,128)S(1)} %copy-done.17, f32[768]{0:T(1024)S(1)} %copy-done.67, f32[768]{0:T(1024)S(1)} %copy-done.57, f32[1024]{0:T(1024)S(1)} %fusion.75, f32[1024]{0:T(1024)S(1)} %broadcast_multiply_fusion), kind=kOutput, calls=%fused_computation.89 | convolution fusion | flops 4838129664 | bytes 14170112 | tf_op jit(solution)/shard_map/dot_general | solution.py:391
  341.9 2.6 copy.94
  351.5 2.7 pad_maximum_fusion.ga
  354.2 80.9 %reduce_all.1 = (f32[4,48,768]{2,1,0:T(8,128)}, f32[4,48,768]{2,1,0:T(8,128)}, f32[4,48,768]{2,1,0:T(8,128)}) custom-call(bf16[4,4,2,2,48,768]{5,4,3,2,1,0:T(8,128)(2,1)} %pad_maximum_fusion.ga, bf16[4,4,2,2,48,768]{5,4,3,2,1,0:T(8,128)(2,1)} %bitcast.247, bf16[4,2,2,4,48,768]{5,4,3,2,1,0:T(8,128)(2,1)} %bitcast.248), custom_call_target="tpu_custom_call" | custom-call | tf_op jit(solution)/shard_map/reduce_all/pallas_call | solution.py:353
  441.2 41.9 %all-reduce = (f32[768]{0:T(1024)}, f32[768]{0:T(1024)}, f32[768]{0:T(1024)}, f32[768]{0:T(1024)}, f32[768]{0:T(1024)}, /*index=5*/f32[768]{0:T(1024)}, f32[768]{0:T(1024)}, f32[3072]{0:T(1024)}, f32[768]{0:T(1024)}) all-reduce(f32[768]{0:T(1024)S(1)} %get-tuple-element.177, ...), channel_id=1, replica_groups=mesh['wide'=16,'narrow'=2] {'wide','narrow'}, use_global_device_ids=true, to_apply=%region_21.22 | all-reduce | flops 9216 | bytes 73728 | tf_op jit(solution)/shard_map/psum | solution.py:580
  483.1 9.4 %add_convert_fusion.2 = bf16[1024,768]{1,0:T(8,128)(2,1)} fusion(f32[1024,768]{1,0:T(8,128)S(1)} %copy-done.17, bf16[1024,3072]{1,0:T(8,128)(2,1)} %get-tuple-element.238, bf16[3072,768]{1,0:T(8,128)(2,1)} %bitcast.283, f32[768]{0:T(1024)S(1)} %copy-done.68), kind=kOutput, calls=%fused_computation.122 | convolution fusion | flops 4834197504 | bytes 15731712 | tf_op jit(solution)/shard_map/dot_general | solution.py:387
  (268 shorter events, 90.5 us)
Async XLA Ops:
  6.3 85.3 %copy-start.26 = (bf16[4,256,768]{2,1,0:T(8,128)(2,1)}, bf16[4,256,768]{2,1,0:T(8,128)(2,1)S(1)}, u32[]{:S(2)}) copy-start(bf16[4,256,768]{2,1,0:T(8,128)(2,1)S(1)} %fusion.68) | copy-start | bytes 4718596
  127.1 8.8 %copy-start = (bf16[2,2,256,12,64]{2,4,3,1,0:T(8,128)(2,1)}, bf16[2,2,256,12,64]{2,4,3,1,0:T(8,128)(2,1)S(1)}, u32[]{:S(2)}) copy-start(bf16[2,2,256,12,64]{2,4,3,1,0:T(8,128)(2,1)S(1)} %get-tuple-element.494) | copy-start | bytes 4718596
  127.1 8.8 %copy-start.42 = (f32[2,2,12,256,1]{3,2,1,4,0:T(8,128)}, f32[2,2,12,256,1]{3,2,1,4,0:T(8,128)S(1)}, u32[]{:S(2)}) copy-start(f32[2,2,12,256,1]{3,2,1,4,0:T(8,128)S(1)} %get-tuple-element.430) | copy-start | bytes 147460
  127.1 8.8 %copy-start.44 = (s32[2,2,256]{2,1,0:T(2,128)}, s32[2,2,256]{2,1,0:T(2,128)S(1)}, u32[]{:S(2)}) copy-start(s32[2,2,256]{2,1,0:T(2,128)S(1)} %get-tuple-element.497) | copy-start | bytes 12292
  127.1 8.8 %copy-start.46 = (s32[2,2,256]{2,1,0:T(2,128)}, s32[2,2,256]{2,1,0:T(2,128)S(1)}, u32[]{:S(2)}) copy-start(s32[2,2,256]{2,1,0:T(2,128)S(1)} %get-tuple-element.498) | copy-start | bytes 12292
  127.1 9.3 %copy-start.2 = (bf16[2,2,256,12,64]{2,4,3,1,0:T(8,128)(2,1)}, bf16[2,2,256,12,64]{2,4,3,1,0:T(8,128)(2,1)S(1)}, u32[]{:S(2)}) copy-start(bf16[2,2,256,12,64]{2,4,3,1,0:T(8,128)(2,1)S(1)} %get-tuple-element.495) | copy-start | bytes 4718596
  137.5 6.7 %copy-start.57 = (f32[768]{0:T(1024)S(1)}, f32[768]{0:T(1024)}, u32[]{:S(2)}) copy-start(f32[768]{0:T(1024)} %param.38) | copy-start | bytes 9220
  137.5 6.7 %copy-start.62 = (f32[3072]{0:T(1024)S(1)}, f32[3072]{0:T(1024)}, u32[]{:S(2)}) copy-start(f32[3072]{0:T(1024)} %param.41) | copy-start | bytes 36868
  137.5 6.7 %copy-start.66 = (f32[768]{0:T(1024)S(1)}, f32[768]{0:T(1024)}, u32[]{:S(2)}) copy-start(f32[768]{0:T(1024)} %param.39) | copy-start | bytes 9220
  144.2 36.9 %copy-start.51 = (s32[4,256]{1,0:T(4,128)S(1)}, s32[4,256]{1,0:T(4,128)}, u32[]{:S(2)}) copy-start(s32[4,256]{1,0:T(4,128)} %param.26) | copy-start | bytes 12292
  144.2 37.0 %copy-start.61 = (s32[4]{0:T(128)S(1)}, s32[4]{0:T(128)}, u32[]{:S(2)}) copy-start(s32[4]{0:T(128)} %param.27) | copy-start | bytes 52
  144.2 82.7 %copy-start.13 = (bf16[4,256,768]{2,1,0:T(8,128)(2,1)S(1)}, bf16[4,256,768]{2,1,0:T(8,128)(2,1)}, u32[]{:S(2)}) copy-start(bf16[4,256,768]{2,1,0:T(8,128)(2,1)} %param.28) | copy-start | bytes 4718596
  223.7 21.9 %copy-start.69 = (s32[3]{0:T(128)}, s32[3]{0:T(128)S(1)}, u32[]{:S(2)}) copy-start(s32[3]{0:T(128)S(1)} %psum.70) | copy-start | bytes 40
  228.0 17.6 %copy-start.16 = (f32[1024,768]{1,0:T(8,128)S(1)}, f32[1024,768]{1,0:T(8,128)}, u32[]{:S(2)}) copy-start(f32[1024,768]{1,0:T(8,128)} %copy-done.15) | copy-start | bytes 9437188
  262.6 6.2 %copy-start.1 = (bf16[2,2,256,12,64]{2,4,3,1,0:T(8,128)(2,1)S(1)}, bf16[2,2,256,12,64]{2,4,3,1,0:T(8,128)(2,1)}, u32[]{:S(2)}) copy-start(bf16[2,2,256,12,64]{2,4,3,1,0:T(8,128)(2,1)} %copy-done) | copy-start | bytes 4718596
  262.6 6.2 %copy-start.43 = (f32[2,2,12,256,1]{3,2,1,4,0:T(8,128)S(1)}, f32[2,2,12,256,1]{3,2,1,4,0:T(8,128)}, u32[]{:S(2)}) copy-start(f32[2,2,12,256,1]{3,2,1,4,0:T(8,128)} %copy-done.42) | copy-start | bytes 147460
  262.6 6.2 %copy-start.45 = (s32[2,2,256]{2,1,0:T(2,128)S(1)}, s32[2,2,256]{2,1,0:T(2,128)}, u32[]{:S(2)}) copy-start(s32[2,2,256]{2,1,0:T(2,128)} %copy-done.44) | copy-start | bytes 12292
  262.6 6.2 %copy-start.47 = (s32[2,2,256]{2,1,0:T(2,128)S(1)}, s32[2,2,256]{2,1,0:T(2,128)}, u32[]{:S(2)}) copy-start(s32[2,2,256]{2,1,0:T(2,128)} %copy-done.46) | copy-start | bytes 12292
  311.8 5.5 %copy-start.7 = (bf16[4,256,768]{2,1,0:T(8,128)(2,1)S(1)}, bf16[4,256,768]{2,1,0:T(8,128)(2,1)}, u32[]{:S(2)}) copy-start(bf16[4,256,768]{2,1,0:T(8,128)(2,1)} %param.24) | copy-start | bytes 4718596
  311.8 5.5 %copy-start.49 = (f32[768]{0:T(1024)S(1)}, f32[768]{0:T(1024)}, u32[]{:S(2)}) copy-start(f32[768]{0:T(1024)} %param.29) | copy-start | bytes 9220
  317.3 6.0 %copy-start.53 = (f32[1,2,4,128]{3,2,1,0:T(4,128)S(1)}, f32[1,2,4,128]{3,2,1,0:T(4,128)}, u32[]{:S(2)}) copy-start(f32[1,2,4,128]{3,2,1,0:T(4,128)} %get-tuple-element.256) | copy-start | bytes 12292
  317.4 10.9 %slice-start.2 = ((s8[6291456]{0:T(1024)(128)(4,1)}), s8[4194304]{0:T(1024)(128)(4,1)S(1)}, s32[]{:S(2)}) async-start(s8[6291456]{0:T(1024)(128)(4,1)} %bitcast.287), calls=%async_computation.2 | async-start | bytes 8388608
  325.7 9.7 %slice-start = ((s8[6291456]{0:T(1024)(128)(4,1)}), s8[4194304]{0:T(1024)(128)(4,1)S(1)}, s32[]{:S(2)}) async-start(s8[6291456]{0:T(1024)(128)(4,1)} %bitcast.285), calls=%async_computation | async-start | bytes 8388608
  328.3 7.2 %copy-start.17 = (f32[1024,768]{1,0:T(8,128)S(1)}, f32[1024,768]{1,0:T(8,128)}, u32[]{:S(2)}) copy-start(f32[1024,768]{1,0:T(8,128)} %copy-done.15) | copy-start | bytes 9437188
  328.3 7.2 %copy-start.67 = (f32[768]{0:T(1024)S(1)}, f32[768]{0:T(1024)}, u32[]{:S(2)}) copy-start(f32[768]{0:T(1024)} %param.39) | copy-start | bytes 9220
  328.3 7.1 %slice-start.1 = ((s8[6291456]{0:T(1024)(128)(4,1)}), s8[2097152]{0:T(1024)(128)(4,1)S(1)}, s32[]{:S(2)}) async-start(s8[6291456]{0:T(1024)(128)(4,1)} %bitcast.285), calls=%async_computation.1 | async-start | bytes 4194304
  435.1 6.1 %copy-start.52 = (f32[768]{0:T(1024)S(1)}, f32[768]{0:T(1024)}, u32[]{:S(2)}) copy-start(f32[768]{0:T(1024)} %get-tuple-element.232) | copy-start | bytes 9220
  435.1 6.1 %copy-start.55 = (f32[3072]{0:T(1024)S(1)}, f32[3072]{0:T(1024)}, u32[]{:S(2)}) copy-start(f32[3072]{0:T(1024)} %get-tuple-element.267) | copy-start | bytes 36868
  435.2 6.1 %copy-start.59 = (f32[768]{0:T(1024)S(1)}, f32[768]{0:T(1024)}, u32[]{:S(2)}) copy-start(f32[768]{0:T(1024)} %get-tuple-element.175) | copy-start | bytes 9220
  435.2 6.0 %copy-start.60 = (f32[768]{0:T(1024)S(1)}, f32[768]{0:T(1024)}, u32[]{:S(2)}) copy-start(f32[768]{0:T(1024)} %get-tuple-element.179) | copy-start | bytes 9220
  435.2 48.0 %copy-start.68 = (f32[768]{0:T(1024)S(1)}, f32[768]{0:T(1024)}, u32[]{:S(2)}) copy-start(f32[768]{0:T(1024)} %param.43) | copy-start | bytes 9220
  483.1 9.4 %copy-start.41 = (f32[4,48,768]{2,1,0:T(8,128)S(1)}, f32[4,48,768]{2,1,0:T(8,128)}, u32[]{:S(2)}) copy-start(f32[4,48,768]{2,1,0:T(8,128)} %get-tuple-element.136) | copy-start | bytes 1769476
  (52 other events, 139.5 us)

commit v2 on v0

v2 whole, which is shorter than its diff:
```python
import functools

import jax
import jax.numpy as jnp
from jax import lax
from jax.experimental import pallas as pl
from jax.experimental.pallas import tpu as pltpu
from jax.sharding import PartitionSpec as P

HEADS = 12
EPSILON = 1e-06
MASKED = -1e30
HALVES = 2
VMEM_BYTES = 63 << 20
TABLE = (
    (0, 0),
    (6,),
    (),
    (6,),
    (),
    (),
    (),
    (6,),
    (),
    (),
    (6, 0, 1, 1, 0, 0, 0, 0, 1, 2, 2, 1, 0, 2, 3, 3, 2, 0, 0),
    (1, 1, 1),
    (),
    (),
    (),
    (),
    (),
    (2, 2, 2),
    (1, 3, 1, 4),
    (4, 3, 1),
    (),
    (),
    (),
    (),
    (2, 2),
    (),
    (2, 3, 3, 3),
    (4, 5),
    (5,),
    (),
    (4,),
    (),
    (),
    (),
    (3, 3),
    (),
    (),
    (3,),
    (4,),
    (),
    (4, 4),
    (),
    (),
    (5,),
    (),
    (),
    (),
    (4,),
    (5,),
    (),
    (),
    (),
    (),
    (),
    (4,),
    (),
    (4,),
    (5, 5),
    (),
    (5,),
    (),
    (7, 7),
    (),
    (5, 5, 7, 5),
    (8, 8),
    (),
    (),
    (7, 7),
    (),
    (),
    (),
    (),
    (),
    (),
    (8,),
    (),
    (),
    (),
    (),
    (),
    (8, 7, 8, 7),
    (),
    (),
    (8,),
    (),
    (7, 8, 7),
    (),
    (),
    (7, 7),
    (8,),
    (9, 9, 8),
    (8,),
    (9,),
    (8,),
    (),
    (),
    (10, 10),
    (),
    (9, 9),
    (),
    (10,),
    (),
    (10, 10),
    (9,),
    (9,),
    (),
    (10, 11, 11),
    (9, 10, 11),
    (9,),
    (),
    (9,),
    (10, 11, 9, 11),
    (10,),
    (10, 12, 12),
    (10, 11),
    (12,),
    (11, 13),
    (11, 12, 12),
    (),
    (11, 13, 11),
    (12, 11, 12, 12, 13, 12, 12, 12, 13),
)

MESH = pl.DeviceIdType.MESH
BF = jnp.bfloat16
F32 = jnp.float32


class Place:
    def __init__(self, depth, lanes):
        wide = lax.axis_index("wide")
        self.depth, self.lanes = depth, lanes
        self.bits = lanes.bit_length() - 1
        self.n = lax.axis_index("narrow")
        self.c = lax.rem(wide, 2)
        self.x = lax.rem(wide // 2, 2)
        self.z = wide // 4
        self.y = lax.rem(self.n, 2)
        self.c_far, self.x_far = 1 - self.c, 1 - self.x
        self.own = (2 * self.y, 2 * self.y + 1)
        self.far = (2 - 2 * self.y, 3 - 2 * self.y)
        self.core = self.at(c=self.c_far)
        self.across_x = self.at(x=self.x_far)
        self.flips = []
        for bit in range(self.bits):
            step = 1 << bit
            low = lax.rem(self.n // step, 2)
            self.flips.append(self.at(n=self.n + step * (1 - 2 * low)))
        self.across_y = self.flips[0]
        self.z_of = [lax.rem(self.z + d, depth) for d in range(depth)]
        self.along_z = [self.at(z=t) for t in self.z_of]

    def at(self, z=None, x=None, c=None, n=None):
        z = self.z if z is None else z
        x = self.x if x is None else x
        c = self.c if c is None else c
        n = self.n if n is None else n
        return ((z * 2 + x) * 2 + c, n)

    def greet(self):
        others = [self.core, self.across_x] + self.flips + self.along_z[1:]
        barrier = pltpu.get_barrier_semaphore()
        for other in others:
            pl.semaphore_signal(barrier, inc=1, device_id=other, device_id_type=MESH)
        pl.semaphore_wait(barrier, len(others))


class Copy:
    def __init__(self, sems, i, src, dst, device):
        self.parts = sems, i, src, dst, device

    def made(self):
        sems, i, src, dst, device = self.parts
        return pltpu.make_async_remote_copy(
            src_ref=src(), dst_ref=dst(), send_sem=sems.send.at[sems.row, i], recv_sem=sems.recv.at[sems.row, i],
            device_id=device, device_id_type=MESH,
        )

    def wait_recv(self):
        self.made().wait_recv()


class Sems:
    def __init__(self, send, recv, row):
        self.send, self.recv, self.row, self.used = send, recv, row, 0
        self.open = []

    def copy(self, src, dst, device):
        copy = Copy(self, self.used, src, dst, device)
        self.used += 1
        copy.made().start()
        self.open.append(copy)
        return copy

    def drain(self):
        for copy in self.open:
            copy.made().wait_send()
        self.open = []


def slot(ref, *at):
    return ref.at[at]


def gather_part(me, sems, view):
    own, far = me.own, me.far
    x, c, z = me.x, me.c, me.z
    every = slice(None)

    def send(u, zs, xs, device):
        block = functools.partial(view, u, zs, xs, c)
        return sems.copy(block, block, device)

    hops = []
    for u in own:
        hops.append([send(u, z, x, me.along_z[d]) for d in range(1, me.depth)])
        yield
    first = []
    for k, u in enumerate(own):
        for hop in hops[k]:
            hop.wait_recv()
        first.append((send(u, every, x, me.across_x), send(u, every, x, me.across_y)))
        yield
    (x_a, y_a), (x_b, y_b) = first
    x_a.wait_recv()
    y_fwd = send(own[0], every, me.x_far, me.across_y)
    cores = [send(own[0], every, every, me.core)]
    yield
    y_b.wait_recv()
    x_fwd = send(far[1], every, x, me.across_x)
    yield
    x_b.wait_recv()
    cores.append(send(own[1], every, every, me.core))
    yield
    y_a.wait_recv()
    y_fwd.wait_recv()
    cores.append(send(far[0], every, every, me.core))
    yield
    x_fwd.wait_recv()
    cores.append(send(far[1], every, every, me.core))
    yield
    for made in cores:
        made.wait_recv()
    yield


def reduce_part(me, sems, view, bufs, emit, credit, wait_credit, give_credit):
    rc, ry, rx, rz, fin, far = [functools.partial(slot, ref, i) for ref, i in bufs]
    (a, b), (ta, tb) = me.own, me.far
    x, c, z = me.x, me.c, me.z
    xo = me.x_far
    every = slice(None)

    def add(dst, *terms):
        total = dst[...].astype(F32)
        for t in terms:
            total = total + t[...].astype(F32)
        dst[...] = total.astype(BF)

    def send(u, zs, xs, device, buf, *at, core=c):
        return sems.copy(functools.partial(view, u, zs, xs, core), functools.partial(buf, *at), device)

    if wait_credit:
        pl.semaphore_wait(credit, 1)
    cores = [send(u, every, every, me.core, rc, i, core=me.c_far) for i, u in enumerate((ta, tb, b, a))]
    yield
    cores[0].wait_recv()
    add(view(ta, every, every, c), rc(0))
    y_diag = send(ta, every, xo, me.across_y, ry, 0)
    yield
    cores[1].wait_recv()
    add(view(tb, every, every, c), rc(1))
    x_diag = send(tb, every, xo, me.across_x, rx, 0)
    yield
    cores[2].wait_recv()
    add(view(b, every, every, c), rc(2))
    x_near = send(b, every, xo, me.across_x, rx, 1)
    y_near = send(ta, every, x, me.across_y, ry, 1)
    cores[3].wait_recv()
    add(view(a, every, every, c), rc(3))
    if give_credit:
        pl.semaphore_signal(credit, inc=1, device_id=me.core, device_id_type=MESH)
    yield
    y_diag.wait_recv()
    add(view(a, every, xo, c), ry(0))
    x_last = send(a, every, xo, me.across_x, rx, 2)
    yield
    x_diag.wait_recv()
    add(view(tb, every, x, c), rx(0))
    y_last = send(tb, every, x, me.across_y, ry, 2)
    yield
    z_hops = []
    y_near.wait_recv()
    x_last.wait_recv()
    add(view(a, every, x, c), ry(1), rx(2))
    z_hops.append([send(a, me.z_of[d], x, me.along_z[d], rz, 0, d - 1) for d in range(1, me.depth)])
    yield
    x_near.wait_recv()
    y_last.wait_recv()
    add(view(b, every, x, c), rx(1), ry(2))
    z_hops.append([send(b, me.z_of[d], x, me.along_z[d], rz, 1, d - 1) for d in range(1, me.depth)])
    yield
    sent = []
    last = max(me.bits - 1, 0)
    for k, u in enumerate((a, b)):
        for hop in z_hops[k]:
            hop.wait_recv()
        total = view(u, z, x, c)[...].astype(F32)
        for d in range(1, me.depth):
            total = total + rz(k, d - 1)[...].astype(F32)
        fin(0, k)[...] = total.astype(BF)
        for bit in range(1, me.bits):
            swap = sems.copy(functools.partial(fin, bit - 1, k), functools.partial(far, bit, k), me.flips[bit])
            swap.wait_recv()
            total = fin(bit - 1, k)[...].astype(F32) + far(bit, k)[...].astype(F32)
            fin(bit, k)[...] = total.astype(BF)
        sent.append(sems.copy(functools.partial(fin, last, k), functools.partial(far, 0, k), me.across_y))
        emit(u, True, k, fin(last, k)[...])
        yield
    for k, u in enumerate((ta, tb)):
        sent[k].wait_recv()
        emit(u, False, k, far(0, k)[...])
        yield


def reduce_copies(depth, lanes):
    bits = lanes.bit_length() - 1
    return 4 + 6 + 2 * (depth - 1) + 2 * (bits - 1) + 2


class Flow:
    def __init__(self, table):
        self.table, self.at, self.parts, self.count = list(table), 0, {}, {}

    def begin(self, i, part):
        self.parts[i], self.count[i] = part, 0

    def step(self, i):
        part = self.parts.get(i)
        if part is not None:
            self.count[i] += 1
            try:
                next(part)
            except StopIteration:
                self.parts[i] = None

    def peek(self, k):
        return self.table[self.at + k] if self.at + k < len(self.table) else ()

    def pump(self):
        for i in self.peek(0):
            self.step(i)
        self.at += 1

    def finish(self, i):
        while self.parts.get(i) is not None:
            self.step(i)

    def finish_all(self):
        while any(part is not None for part in self.parts.values()):
            for i in list(self.parts):
                self.step(i)


def stepped(flow, total, work):
    @pl.loop(0, total)
    def _(i):
        work(i)
        for k in range(total):
            if flow.peek(0):
                pl.when(i == k)(flow.pump)
            else:
                flow.pump()


def gather_copies(depth):
    return 2 * (depth - 1) + 4 + 2 + 4


GATHER_STEPS = 10


def all_sum(me, sems, first, pairs, stack, emit):
    hops = [me.core, me.across_x] + me.flips
    have = functools.partial(slot, first, slice(None))
    for i, other in enumerate(hops):
        came, total = functools.partial(slot, pairs, 2 * i), functools.partial(slot, pairs, 2 * i + 1)
        made = sems.copy(have, came, other)
        yield
        made.wait_recv()
        total()[...] = have()[...] + came()[...]
        have = total
    stack[me.z] = have()[...]
    mine = functools.partial(slot, stack, me.z)
    made = [sems.copy(have, mine, me.along_z[d]) for d in range(1, me.depth)]
    yield
    for m in made:
        m.wait_recv()
    total = stack[0]
    for i in range(1, me.depth):
        total = total + stack[i]
    emit(total)
    yield


def all_sum_sizes(depth, lanes):
    hops = 2 + lanes.bit_length() - 1
    return 2 * hops, hops + depth - 1, hops + 2


class Row:
    def __init__(self, ref):
        self.ref = ref

    def __getitem__(self, at):
        if at is Ellipsis:
            return self.ref[...].reshape(1, -1)
        return self.ref[at[1]].reshape(1, -1)


def stats(values):
    mean = jnp.mean(values, axis=-1, keepdims=True)
    centred = values - mean
    rstd = lax.rsqrt(jnp.mean(centred * centred, axis=-1, keepdims=True) + EPSILON)
    return centred, rstd


def dot_nn(a, b):
    return jnp.dot(a, b, preferred_element_type=F32)


def dot_nt(a, b):
    return lax.dot_general(a, b, (((1,), (1,)), ((), ())), preferred_element_type=F32)


def dot_tn(a, b):
    return lax.dot_general(a, b, (((0,), (0,)), ((), ())), preferred_element_type=F32)


def lane_halves(width=128):
    lane = lax.broadcasted_iota(jnp.int32, (1, width), 1)
    low = (lane < width // 2).astype(F32)
    return low.astype(BF), (1.0 - low).astype(BF)


def norm_back(grad, normed, rstd):
    mean_g = jnp.mean(grad, axis=-1, keepdims=True)
    mean_gn = jnp.mean(grad * normed, axis=-1, keepdims=True)
    return (grad - mean_g - normed * mean_gn) * rstd


def down_sum(values):
    return jnp.sum(values, axis=0, keepdims=True)


def layer_kernel(
    depth, lanes, halves,
    x_h, cot_h, seg, live, expert, g1, b1, qb, vb, ob, g2, b2, ib, yb,
    q_w, k_w, v_w, o_w, w_in, w_out,
    out_h, dx_h, counts, d_q, d_k, d_v, d_o, d_in, d_out,
    d_g1, d_b1, d_qb, d_vb, d_ob, d_g2, d_b2, d_ib, d_yb,
    qkv_h, a_h, pb_h, z_h, h_h,
    ga, gi, go, s1, s2, pa, po, x_s, o_s, c_s, xh, dattn, hd, tok, rstd_s,
    rc, ry, rx, rz, fin, far, vec, vec_pair, vec_stack, cnt, cnt_pair, cnt_stack, ib_s,
    local, send, recv, rsend, rrecv, csend, crecv, vsend, vrecv, credit,
):
    me = Place(depth, lanes)
    g1, b1, qb, vb, ob, g2, b2, ib, yb = [Row(t) for t in (g1, b1, qb, vb, ob, g2, b2, ib, yb)]
    rows_w, width = q_w.shape
    row_total, slots = seg.shape
    blocks = s1.shape[0]
    x_, c_, z_ = me.x, me.c, me.z
    part = width // halves
    pairs_half = part // 128
    per = depth // 4
    part_total = 3 * halves
    used = [2]

    def move(src, dst):
        made = pltpu.make_async_copy(src, dst, local.at[used[0]])
        used[0] += 1
        made.start()
        return made

    def row(r):
        return pl.ds(pl.multiple_of(r * slots, slots), slots)

    def fill(refs):
        for k, ref in enumerate(refs):
            pltpu.make_async_copy(ref, ga.at[me.own[k], z_, x_, c_], local.at[k]).start()

    @pl.when(me.y == 0)
    def _():
        fill((q_w, k_w))

    @pl.when(me.y == 1)
    def _():
        fill((v_w, o_w))

    filled = [pltpu.make_async_copy(q_w, ga.at[me.own[k], z_, x_, c_], local.at[k]) for k in range(2)]
    for u in me.own:
        filled.append(move(w_in.at[:, pl.ds(pl.multiple_of(u * width, width), width)], gi.at[u, z_, x_, c_]))
        filled.append(move(w_out.at[pl.ds(pl.multiple_of(u * rows_w, 8), rows_w), :], go.at[z_, x_, c_, u]))
    m_x = move(x_h, x_s)
    gb = x_s
    me.greet()
    for m in filled:
        m.wait()

    def view_of(g, h, first, second, third):
        cols = pl.ds(h * part, part)

        def view(u, zs, xs, cs):
            if g == 2:
                return third.at[zs, xs, cs, u, :, cols]
            return (first, second)[g].at[u, zs, xs, cs, :, cols]

        return view

    flow, gather_sems, reduce_sems = Flow(TABLE), [], []
    for g in range(3):
        for h in range(halves):
            sems = Sems(send, recv, g * halves + h)
            gather_sems.append(sems)
            flow.begin(g * halves + h, gather_part(me, sems, view_of(g, h, ga, gi, go)))
    flow.pump()
    m_cot = move(cot_h, dattn)
    vec[...] = jnp.zeros_like(vec)
    for u in range(blocks):
        ib_s[u : u + 1, :] = ib[:, pl.ds(u * width, width)]

    def ready(i):
        flow.pump()
        flow.finish(i)

    cnt[...] = jnp.zeros_like(cnt)
    for r in range(row_total):
        for e in range(3):
            hit = (expert[r] == e).astype(jnp.int32)
            cnt[e : e + 1, :] += live[r : r + 1, :] * hit
    csems = Sems(csend, crecv, 0)

    def count_out(total):
        summed = jnp.broadcast_to(jnp.sum(total, axis=1, keepdims=True), (8, 128))
        for e in range(3):
            counts[e] = jnp.sum(total[e : e + 1, :].astype(F32)).astype(jnp.int32)
        one = [summed[e : e + 1, :].astype(F32) for e in range(3)]
        for r in range(row_total):
            own = jnp.zeros_like(one[0])
            for e in range(3):
                own = own + one[e] * (expert[r] == e).astype(F32)
            scale = (one[1] + one[2]) / (2.0 * own)
            rows = pl.ds(r * slots, slots)
            tok[rows, :] = tok[rows, :] * scale

    flow.begin(part_total, all_sum(me, csems, cnt, cnt_pair, cnt_stack, count_out))
    flow.pump()
    m_x.wait()

    def first_norm(r):
        rows = row(r)
        centred, rstd = stats(x_s[rows, :].astype(F32))
        s1[3, rows, :] = (centred * rstd * g1[...] + b1[...]).astype(BF)

    stepped(flow, row_total, first_norm)
    m_a = move(s1.at[3], a_h)

    row_pos = lax.broadcasted_iota(jnp.int32, (slots, slots), 0)
    col_pos = lax.broadcasted_iota(jnp.int32, (slots, slots), 1)
    for r in range(row_total):
        seg_row = seg[r : r + 1, :]
        live_row = live[r : r + 1, :]
        down = jnp.transpose(jnp.broadcast_to(seg_row.astype(F32), (slots, slots)))
        across = jnp.where(live_row > 0, seg_row, -1 - col_pos[0:1, :]).astype(F32)
        allowed = (down == across) | (row_pos == col_pos)
        hd[pl.ds(r * slots, slots), pl.ds(0, slots)] = jnp.where(allowed, 0.0, MASKED)
        live_down = jnp.transpose(jnp.broadcast_to(live_row.astype(F32), (128, slots)))
        tok[pl.ds(r * slots, slots), :] = live_down
        flow.pump()

    masks = lane_halves()
    for h in range(halves):
        cols_h = pl.ds(h * part, part)
        ready(h)

        def project(r):
            rows = row(r)
            a_row = s1[3, rows, :]
            for u, add in enumerate((qb, None, vb)):
                value = dot_nn(a_row, ga[u, :, :, :, :, cols_h].reshape(width, part))
                if add is not None:
                    value = value + add[:, cols_h]
                s1[u, rows, cols_h] = value.astype(BF)

        stepped(flow, row_total, project)

        def attend(r):
            rows = row(r)
            for p in range(pairs_half):
                cols = pl.ds(h * part + p * 128, 128)
                q2, k2, v2 = s1[0, rows, cols], s1[1, rows, cols], s1[2, rows, cols]
                mixed = jnp.zeros((slots, 128), F32)
                for i in range(2):
                    scores = dot_nt(q2 * (masks[i] * 0.125), k2) + hd[rows, pl.ds(0, slots)]
                    top = jnp.max(scores, axis=-1, keepdims=True)
                    terms = jnp.exp(scores - top)
                    inv = 1.0 / jnp.sum(terms, axis=-1, keepdims=True)
                    probs = (terms * inv).astype(BF)
                    head = (h * pairs_half + p) * 2 + i
                    s2[head // 3, rows, pl.ds((head % 3) * slots, slots)] = probs
                    mixed = mixed + dot_nn(probs, v2 * masks[i])
                o_s[rows, cols] = mixed.astype(BF)

        stepped(flow, row_total, attend)
    m_qkv = [move(s1.at[u], qkv_h.at[u]) for u in range(3)]
    m_pb = move(s2, pb_h)

    def second_norm(r):
        rows = row(r)
        h_row = x_s[rows, :].astype(F32) + dot_nn(o_s[rows, :], ga[3].reshape(width, width)) + ob[...]
        hd[rows, :] = h_row
        centred, rstd = stats(h_row)
        normed = centred * rstd
        xh[rows, :] = normed.astype(BF)
        rstd_s[rows, :] = jnp.broadcast_to(rstd, (slots, 128))
        c_s[rows, :] = (normed * g2[...] + b2[...]).astype(BF)

    stepped(flow, row_total, second_norm)
    m_h = move(hd, h_h)
    for m in (m_a, *m_qkv, m_pb):
        m.wait()
    pair_rows = row_total // 2
    for h in range(halves):
        cols_h = pl.ds(h * part, part)
        ready(halves + h)

        def hidden(t):
            u, first = t // pair_rows, 2 * lax.rem(t, pair_rows)
            weight = gi[u, :, :, :, :, cols_h].reshape(width, part)
            for s in range(2):
                rows = row(first + s)
                pre = dot_nn(c_s[rows, :], weight) + ib_s[pl.ds(u, 1), cols_h]
                cdf = 0.5 * (1.0 + lax.erf(pre * 0.7071067811865476))
                s1[u, rows, cols_h] = (pre * cdf).astype(BF)
                s2[u, rows, cols_h] = (cdf + pre * (jnp.exp(-0.5 * pre * pre) * 0.3989422804014327)).astype(BF)

        stepped(flow, blocks * pair_rows, hidden)
    m_z = move(s1, z_h)
    flow.finish(part_total)
    m_cot.wait()

    def begin(g, h, i):
        cols = pl.ds(h * part, part)

        def emit(u, mine, k, value):
            value = value.astype(F32)
            if g == 0:
                even = (me.y == 0) if mine else (me.y == 1)

                @pl.when(even)
                def _():
                    (d_q, d_k)[k][:, cols] = value

                @pl.when(jnp.logical_not(even))
                def _():
                    (d_v, d_o)[k][:, cols] = value
            elif g == 1:
                d_in[:, pl.ds(pl.multiple_of(u * width + h * part, 128), part)] = value
            else:
                d_out[pl.ds(pl.multiple_of(u * rows_w, 8), rows_w), cols] = value

        sems = Sems(rsend, rrecv, i)
        reduce_sems.append(sems)
        bufs = [(rc, i % 2)] + [(t, i) for t in (ry, rx, rz, fin, far)]
        base = part_total + 1
        while i >= 2 and flow.count[base + i - 2] < 4:
            flow.step(base + i - 2)
        view = view_of(g, h, pa, gi, po)
        flow.begin(base + i, reduce_part(me, sems, view, bufs, emit, credit, i >= 2, i < part_total - 2))
        flow.step(base + i)

    def scaled(r):
        rows = row(r)
        value = (dattn[rows, :].astype(F32) * tok[rows, 0:1]).astype(BF)
        gb[rows, :] = value
        vec[7:8, :] += down_sum(value.astype(F32))

    stepped(flow, row_total, scaled)
    for h in range(halves):
        cols_h = pl.ds(h * part, part)

        def out_grad(u):
            value = dot_tn(s1[u], gb[:, cols_h]).astype(BF)
            po[pl.ds(u * per, per), :, :, :, :, cols_h] = value.reshape(per, 2, 2, 4, rows_w, part)

        stepped(flow, blocks, out_grad)
        begin(2, h, h)
    m_z.wait()
    m_q = [move(qkv_h.at[u], s1.at[u]) for u in range(3)] + [move(a_h, s1.at[3])]
    for h in range(halves):
        ready(2 * halves + h)

    def hidden_grad(t):
        u, rows = t // row_total, row(lax.rem(t, row_total))
        weight = go[pl.ds(u * per, per)].reshape(width, width)
        value = (dot_nt(gb[rows, :], weight) * s2[u, rows, :].astype(F32)).astype(BF)
        s2[u, rows, :] = value
        vec[pl.ds(8 + u, 1), :] += down_sum(value.astype(F32))

    stepped(flow, blocks * row_total, hidden_grad)
    m_h.wait()

    def mid_grad(r):
        rows = row(r)
        grad = dot_nt(s2[0, rows, :], gi[0].reshape(width, width))
        for u in range(1, blocks):
            grad = grad + dot_nt(s2[u, rows, :], gi[u].reshape(width, width))
        normed = xh[rows, :].astype(F32)
        vec[5:6, :] += down_sum(grad * normed)
        vec[6:7, :] += down_sum(grad)
        value = dattn[rows, :].astype(F32) * tok[rows, 0:1]
        value = value + norm_back(grad * g2[...], normed, rstd_s[rows, 0:1])
        hd[rows, :] = value
        value = value.astype(BF)
        dattn[rows, :] = value
        vec[4:5, :] += down_sum(value.astype(F32))

    stepped(flow, row_total, mid_grad)
    for s in gather_sems:
        s.drain()
    csems.drain()
    for h in range(halves):
        cols_h = pl.ds(h * part, part)

        def in_grad(u):
            value = dot_tn(c_s[...], s2[u, :, cols_h]).astype(BF)
            gi[u, :, :, :, :, cols_h] = value.reshape(depth, 2, 2, rows_w, part)

        stepped(flow, blocks, in_grad)
        begin(1, h, halves + h)
    m_p = move(pb_h, s2)
    for h in range(halves):
        cols_h = pl.ds(h * part, part)
        value = dot_tn(o_s[...], dattn[:, cols_h]).astype(BF)
        pa[3, :, :, :, :, cols_h] = value.reshape(depth, 2, 2, rows_w, part)
        flow.pump()

    def mixed_grad(r):
        rows = row(r)
        gb[rows, :] = dot_nt(dattn[rows, :], ga[3].reshape(width, width)).astype(BF)

    stepped(flow, row_total, mixed_grad)
    for m in m_q:
        m.wait()
    m_p.wait()
    for h in range(halves):
        cols_h = pl.ds(h * part, part)

        def attend_back(r):
            rows = row(r)
            for p in range(pairs_half):
                cols = pl.ds(h * part + p * 128, 128)
                q2, k2, v2, do2 = s1[0, rows, cols], s1[1, rows, cols], s1[2, rows, cols], gb[rows, cols]
                dq = jnp.zeros((slots, 128), F32)
                dk, dv = dq, dq
                for i in range(2):
                    head = (h * pairs_half + p) * 2 + i
                    probs = s2[head // 3, rows, pl.ds((head % 3) * slots, slots)]
                    do1 = do2 * masks[i]
                    dp = dot_nt(do1, v2)
                    wide = probs.astype(F32)
                    inner = jnp.sum(dp * wide, axis=-1, keepdims=True)
                    ds = (wide * (dp - inner)).astype(BF)
                    dq = dq + dot_nn(ds, k2 * masks[i])
                    dk = dk + dot_tn(ds, q2 * masks[i])
                    dv = dv + dot_tn(probs, do1)
                dq, dv = (dq * 0.125).astype(BF), dv.astype(BF)
                s1[0, rows, cols] = dq
                s1[1, rows, cols] = (dk * 0.125).astype(BF)
                s1[2, rows, cols] = dv
                vec[2:3, cols] += down_sum(dq.astype(F32))
                vec[3:4, cols] += down_sum(dv.astype(F32))

        stepped(flow, row_total, attend_back)
        if h == halves - 1:
            m_x = move(x_h, x_s)

        def project_grad(u):
            value = dot_tn(s1[3], s1[u, :, cols_h]).astype(BF)
            pa[u, :, :, :, :, cols_h] = value.reshape(depth, 2, 2, rows_w, part)

        stepped(flow, 3, project_grad)
        begin(0, h, 2 * halves + h)
    m_z = move(z_h, s2)
    m_x.wait()

    def last_grad(r):
        rows = row(r)
        grad = dot_nt(s1[0, rows, :], ga[0].reshape(width, width))
        for u in (1, 2):
            grad = grad + dot_nt(s1[u, rows, :], ga[u].reshape(width, width))
        centred, rstd = stats(x_s[rows, :].astype(F32))
        normed = centred * rstd
        vec[0:1, :] += down_sum(grad * normed)
        vec[1:2, :] += down_sum(grad)
        dattn[rows, :] = (hd[rows, :] + norm_back(grad * g1[...], normed, rstd)).astype(BF)

    stepped(flow, row_total, last_grad)
    m_h = move(h_h, hd)
    m_dx = move(dattn, dx_h)
    vsems = Sems(vsend, vrecv, 0)

    def vec_out(total):
        for i, ref in enumerate((d_g1, d_b1, d_qb, d_vb, d_ob, d_g2, d_b2, d_yb)):
            ref[...] = total[i]
        for u in range(blocks):
            d_ib[pl.ds(u * width, width)] = total[8 + u]

    vec_part = 2 * part_total + 1
    flow.begin(vec_part, all_sum(me, vsems, vec, vec_pair, vec_stack, vec_out))
    flow.step(vec_part)
    m_z.wait()
    m_h.wait()

    def outward(r):
        rows = row(r)
        value = hd[rows, :] + yb[...]
        for u in range(blocks):
            value = value + dot_nn(s2[u, rows, :], go[u * per : (u + 1) * per].reshape(width, width))
        gb[rows, :] = value.astype(BF)

    stepped(flow, row_total, outward)
    m_out = move(gb, out_h)
    flow.pump()
    flow.finish_all()
    for s in reduce_sems:
        s.drain()
    vsems.drain()
    m_dx.wait()
    m_out.wait()


def whole_layer(depth, lanes, halves, x, cot, seg, live, expert, vectors, weights):
    tokens, width = x.shape
    row_total, slots = seg.shape
    rows_w = weights[0].shape[0]
    ff = weights[4].shape[1]
    blocks = ff // width
    parts, cols = 3 * halves, width // halves
    g_per, r_per = gather_copies(depth), reduce_copies(depth, lanes)
    bits = max(lanes.bit_length() - 1, 1)
    pair_n, pair_c, _ = all_sum_sizes(depth, lanes)
    vec_rows = 8 + -(-blocks // 8) * 8
    anyspec = pl.BlockSpec(memory_space=pl.ANY)
    vspec = pl.BlockSpec(memory_space=pltpu.VMEM)
    sspec = pl.BlockSpec(memory_space=pltpu.SMEM)
    like = jax.ShapeDtypeStruct
    unit, unit_o = (4, depth, 2, 2, rows_w, width), (depth, 2, 2, 4, rows_w, width)
    flat, wide = (tokens, width), (blocks, tokens, width)
    o = lambda *s: like(s, F32)
    v = lambda *s: pltpu.VMEM(s, BF)
    f = lambda *s: pltpu.VMEM(s, F32)
    n = lambda *s: pltpu.VMEM(s, jnp.int32)
    dma = lambda *s: pltpu.SemaphoreType.DMA(s)
    return pl.pallas_call(
        functools.partial(layer_kernel, depth, lanes, halves),
        out_shape=[like(flat, BF), like(flat, BF), like((3,), jnp.int32)]
        + [o(rows_w, width)] * 4 + [o(rows_w, ff), o(4 * rows_w, width)]
        + [o(width)] * 7 + [o(ff), o(width)]
        + [like((3, *flat), BF), like(flat, BF), like(wide, BF), like(wide, BF), like(flat, F32)],
        in_specs=[anyspec] * 2 + [vspec] * 2 + [sspec] + [vspec] * 9 + [anyspec] * 6,
        out_specs=[anyspec] * 2 + [sspec] + [vspec] * 15 + [anyspec] * 5,
        scratch_shapes=[
            v(*unit), v(*unit), v(*unit_o), v(*wide), v(*wide), v(*unit), v(*unit_o),
            v(*flat), v(*flat), v(*flat), v(*flat), v(*flat), f(*flat), f(tokens, 128), f(tokens, 128),
            v(2, 4, depth, 2, rows_w, cols), v(parts, 3, depth, rows_w, cols), v(parts, 3, depth, rows_w, cols),
            v(parts, 2, depth - 1, rows_w, cols), v(parts, bits, 2, rows_w, cols), v(parts, bits, 2, rows_w, cols),
            f(vec_rows, width), f(pair_n, vec_rows, width), f(depth, vec_rows, width),
            n(8, slots), n(pair_n, 8, slots), n(depth, 8, slots), f(-(-blocks // 8) * 8, width),
            dma(40), dma(parts, g_per), dma(parts, g_per), dma(parts, r_per), dma(parts, r_per),
            dma(1, pair_c), dma(1, pair_c), dma(1, pair_c), dma(1, pair_c), pltpu.SemaphoreType.REGULAR,
        ],
        compiler_params=pltpu.CompilerParams(collective_id=0, has_side_effects=True, vmem_limit_bytes=VMEM_BYTES),
        name="whole_layer",
    )(x, cot, seg, live, expert, *vectors, *weights)


def hand_over_kernel(count, *refs):
    sources, targets = refs[:count], refs[count + 1 : 2 * count + 1]
    stage, sem = refs[2 * count + 2 : 3 * count + 2], refs[-1]
    into = [pltpu.make_async_copy(s, m, sem.at[0, i]) for i, (s, m) in enumerate(zip(sources, stage))]
    out = [pltpu.make_async_copy(m, t, sem.at[1, i]) for i, (m, t) in enumerate(zip(stage, targets))]
    for m in into:
        m.start()
    for i in range(3):
        refs[2 * count + 1][i] = refs[count][i]
    for first, second in zip(into, out):
        first.wait()
        second.start()
    for m in out:
        m.wait()


def hand_over(counts, arrays):
    anyspec = pl.BlockSpec(memory_space=pl.ANY)
    sspec = pl.BlockSpec(memory_space=pltpu.SMEM)
    count = len(arrays)
    return pl.pallas_call(
        functools.partial(hand_over_kernel, count),
        out_shape=[jax.ShapeDtypeStruct(t.shape, t.dtype) for t in (*arrays, counts)],
        in_specs=[anyspec] * count + [sspec],
        out_specs=[anyspec] * count + [sspec],
        scratch_shapes=[pltpu.VMEM(t.shape, t.dtype) for t in arrays] + [pltpu.SemaphoreType.DMA((2, count))],
        name="hand_over",
    )(*arrays, counts)


def body(
    layer_in, segment_ids, live_mask, expert_ids, cotangent,
    norm1_gain, norm1_bias, q_weight, q_bias, k_weight, v_weight, v_bias, o_weight, o_bias,
    norm2_gain, norm2_bias, in_weight, in_bias, out_weight, out_bias,
):
    row_local, slot_total, width_all = layer_in.shape
    tokens = row_local * slot_total
    depth = lax.axis_size("wide") // 4
    lanes = lax.axis_size("narrow")
    x = layer_in.reshape(tokens, width_all)
    vectors = [norm1_gain, norm1_bias, q_bias, v_bias, o_bias, norm2_gain, norm2_bias, in_bias, out_bias]
    weights = (q_weight, k_weight, v_weight, o_weight, in_weight, out_weight)
    layer_out, input_grad, counts, *grads = whole_layer(
        depth, lanes, HALVES, x, cotangent.reshape(tokens, width_all), segment_ids, live_mask, expert_ids, vectors, weights
    )
    (
        layer_out, input_grad, d_q, d_k, d_v, d_o, d_in, d_out,
        d_g1, d_b1, d_qb, d_vb, d_ob, d_g2, d_b2, d_ib, d_yb, counts,
    ) = hand_over(counts, (layer_out, input_grad, *grads[:15]))
    return (
        layer_out.reshape(layer_in.shape), input_grad.reshape(layer_in.shape), counts,
        d_g1, d_b1, d_q, d_qb, d_k, d_v, d_vb, d_o, d_ob, d_g2, d_b2, d_in, d_ib, d_out, d_yb,
    )


def solution(mesh):
    rows, row_pair = P(("wide", "narrow"), None, None), P(("wide", "narrow"), None)
    whole, split = P(), P("wide", None)
    return jax.shard_map(
        body,
        mesh=mesh,
        in_specs=(
            rows, row_pair, row_pair, P(("wide", "narrow")), rows,
            whole, whole, split, whole, split, split, whole, split, whole,
            whole, whole, split, whole, split, whole,
        ),
        out_specs=(
            rows, rows, whole, whole, whole, split, whole, split, split, whole, split, whole,
            whole, whole, split, whole, split, whole,
        ),
        check_vma=False,
    )
```

time: 785 us -> 179 us (0.23); the launches traced: 776 us -> 179 us
  waiting for transfers between devices: 405 us -> 0 us
  Pallas kernels: 0 us -> 178 us
  matrix products: 162 us -> 0 us
  blocking collectives: 83.7 us -> 0 us
  local copies, waits for them, and re-layouts: 65.4 us -> 0 us
  other arithmetic: 42.9 us -> 0 us
  between operations: 16.1 us -> 0.85 us
    reduce_scatter x6 -> x0, waiting for transfers between devices: 287 us -> none  [the longest x1 78.8 us: body(): lax.psum_scatter(out_weight_grad.astype(jnp.bfloat16), 'wide', scatter_di...]
    pallas_call x0 -> x2, Pallas kernels: none -> 178 us  [the longest x1 173 us: whole_layer(): pl.pallas_call(functools.partial(layer_kernel, depth, lanes, halves), out...]
    dot_general x32 -> x0, matrix products: 162 us -> none  [the longest x6 59.2 us: plain_product(): return jnp.dot(left, right, preferred_element_type=jnp.float32)]
    all_gather x6 -> x0, waiting for transfers between devices: 114 us -> none  [the longest x1 48.2 us: body(): lax.all_gather(in_weight, 'wide', axis=0, tiled=True)]
    psum x2 -> x0, blocking collectives: 83.7 us -> none  [the longest x1 42.4 us: body(): counts = lax.psum(local_counts, ('wide', 'narrow'))]
    convert_element_type x13 -> x0, other arithmetic: 22.3 us -> none  [the longest x1 4.51 us: body(): (grad_resid + grad_x_norm).astype(jnp.bfloat16)]
    reshape x10 -> x0, local copies, waits for them, and re-layouts: 22 us -> none  [the longest x4 11.3 us: heads_blocks(): return values.reshape(block_total, group_rows, slot_total, HEADS, head_dim)]
    reduce_sum x12 -> x0, other arithmetic: 14.9 us -> none  [the longest x1 3.16 us: norm_rows(): return centred * lax.rsqrt(variance + EPSILON) * gain_vec + bias_vec]
  transfers between devices with their start and end apart: 13 -> 0, of which waited for: 10 -> 0; matrix products, arithmetic and copies ran while one was open for 28% -> 0% of each run, Pallas kernels for 0% -> 0%
where the time goes in v2:
time: 179 us
  Pallas kernels  178 us (99%)
    pallas_call x1, Pallas kernels, whole_layer(): pl.pallas_call(functools.partial(layer_kernel, depth, lanes, halves), out...  173 us
    pallas_call x1, Pallas kernels, hand_over(): pl.pallas_call(functools.partial(hand_over_kernel, count), out_shape=[jax...  5.2 us

profile of v2, /device:TPU:0, one launch (start us, length us, event | category | flops | bytes accessed | tf_op | source)
XLA Modules:
  0.0 179.2 jit_solution(18289551886611701713)
XLA Ops:
  0.7 173.2 %whole_layer.1 = (bf16[1024,768]{1,0:T(8,128)(2,1)}, bf16[1024,768]{1,0:T(8,128)(2,1)}, s32[3]{0:T(128)}, f32[48,768]{1,0:T(8,128)}, f32[48,768]{1,0:T(8,128)}, ...) custom-call(bf16[1024,768]{1,0:T(8,128)(2,1)} %bitcast.4, ...), custom_call_target="tpu_custom_call" | custom-call | tf_op jit(solution)/shard_map/whole_layer/pallas_call | solution.py:880
  173.9 5.2 %hand_over.1 = (bf16[1024,768]{1,0:T(8,128)(2,1)}, bf16[1024,768]{1,0:T(8,128)(2,1)}, f32[48,768]{1,0:T(8,128)}, f32[48,768]{1,0:T(8,128)}, f32[48,768]{1,0:T(8,...) custom-call(bf16[1024,768]{1,0:T(8,128)(2,1)} %get-tuple-element.54., ...), custom_call_target="tpu_custom_call" | custom-call | tf_op jit(solution)/shard_map/hand_over/pallas_call | solution.py:923

commit v3 on v2

--- a/solution.py
+++ b/solution.py
@@ -10,130 +10,169 @@
 HEADS = 12
 EPSILON = 1e-06
 MASKED = -1e30
-HALVES = 2
+GATHER_CUTS = ((2, 2, 2), (2, 2, 2), (3, 3))
+REDUCE_CUTS = ((3, 3), (3, 3), (2, 2, 1, 1))
 VMEM_BYTES = 63 << 20
 TABLE = (
     (0, 0),
+    (8,),
+    (),
+    (),
+    (8,),
+    (),
+    (),
+    (),
+    (8,),
+    (),
+    (0, 1, 1, 0, 8, 0, 0, 0, 1, 2, 2, 1, 0, 2, 3, 3, 2, 0, 0),
+    (1, 1, 1),
+    (),
+    (),
+    (),
+    (),
+    (3, 4, 4),
+    (2, 2, 2),
+    (),
+    (3, 1, 1, 1),
+    (),
+    (),
+    (4, 5, 5),
+    (),
+    (3,),
+    (2, 2),
+    (3, 4, 3),
+    (2,),
+    (),
+    (4,),
+    (),
+    (),
+    (),
+    (5, 6),
+    (3, 6),
+    (3, 5),
+    (4, 4),
+    (3, 5),
+    (4,),
+    (),
+    (6, 7),
+    (),
+    (),
+    (4, 7),
+    (5, 5),
+    (),
+    (4,),
+    (),
+    (5, 6),
+    (),
+    (),
+    (),
+    (),
+    (),
+    (),
+    (),
+    (),
+    (),
+    (7,),
+    (5, 6, 7, 6, 5),
+    (),
+    (),
+    (),
+    (),
+    (),
+    (),
+    (),
     (6,),
     (),
-    (6,),
-    (),
-    (),
-    (),
-    (6,),
-    (),
-    (),
-    (6, 0, 1, 1, 0, 0, 0, 0, 1, 2, 2, 1, 0, 2, 3, 3, 2, 0, 0),
-    (1, 1, 1),
-    (),
-    (),
-    (),
-    (),
-    (),
-    (2, 2, 2),
-    (1, 3, 1, 4),
-    (4, 3, 1),
-    (),
-    (),
-    (),
-    (),
-    (2, 2),
-    (),
-    (2, 3, 3, 3),
-    (4, 5),
-    (5,),
-    (),
-    (4,),
-    (),
-    (),
-    (),
-    (3, 3),
-    (),
-    (),
-    (3,),
-    (4,),
-    (),
-    (4, 4),
-    (),
-    (),
-    (5,),
-    (),
-    (),
-    (),
-    (4,),
-    (5,),
-    (),
-    (),
-    (),
-    (),
-    (),
-    (4,),
-    (),
-    (4,),
-    (5, 5),
-    (),
-    (5,),
-    (),
-    (7, 7),
-    (),
-    (5, 5, 7, 5),
-    (8, 8),
-    (),
-    (),
-    (7, 7),
-    (),
-    (),
-    (),
-    (),
-    (),
-    (),
-    (8,),
-    (),
-    (),
-    (),
-    (),
-    (),
-    (8, 7, 8, 7),
-    (),
-    (),
-    (8,),
-    (),
-    (7, 8, 7),
-    (),
-    (),
-    (7, 7),
-    (8,),
-    (9, 9, 8),
-    (8,),
-    (9,),
-    (8,),
+    (),
+    (),
+    (),
+    (),
+    (),
+    (),
+    (),
+    (6, 7, 7),
+    (),
+    (6, 7),
+    (9, 9),
+    (9, 6),
+    (7, 7, 10, 10, 10, 7),
+    (),
+    (),
+    (),
+    (),
+    (),
+    (),
+    (),
+    (),
+    (),
+    (),
+    (),
+    (9, 9),
+    (),
+    (),
+    (),
     (),
     (),
     (10, 10),
     (),
+    (),
     (9, 9),
     (),
-    (10,),
-    (),
-    (10, 10),
-    (9,),
-    (9,),
-    (),
-    (10, 11, 11),
-    (9, 10, 11),
-    (9,),
-    (),
-    (9,),
-    (10, 11, 9, 11),
-    (10,),
-    (10, 12, 12),
+    (11, 11),
+    (),
     (10, 11),
+    (10, 11, 12),
+    (9, 9),
+    (12, 11),
+    (),
+    (),
+    (),
+    (9, 9, 10, 11, 10),
+    (),
+    (),
+    (),
     (12,),
-    (11, 13),
-    (11, 12, 12),
-    (),
-    (11, 13, 11),
-    (12, 11, 12, 12, 13, 12, 12, 12, 13),
+    (),
+    (10, 12, 10),
+    (12,),
+    (),
+    (11, 11),
+    (),
+    (),
+    (12,),
+    (13, 13, 13),
+    (11, 12, 11),
+    (),
+    (),
+    (12,),
+    (),
+    (11,),
+    (),
+    (12, 13, 13),
+    (12,),
+    (14, 14),
+    (),
+    (),
+    (),
+    (14, 12),
+    (),
+    (),
+    (13,),
+    (15, 15),
+    (),
+    (13, 15, 16, 16),
+    (13, 14, 14),
+    (15,),
+    (13, 15),
+    (13, 16, 17, 16),
+    (14, 15, 16),
+    (),
+    (13, 14),
+    (15,),
+    (15, 16, 17),
+    (16,),
+    (),
+    (14, 17, 15, 15, 16, 14, 14, 15, 16, 16, 16, 14, 17),
 )
 
 MESH = pl.DeviceIdType.MESH
@@ -217,6 +256,10 @@
     return ref.at[at]
 
 
+def strip(ref, cols, *at):
+    return ref.at[(*at, *[slice(None)] * (len(ref.shape) - 1 - len(at)), cols)]
+
+
 def gather_part(me, sems, view):
     own, far = me.own, me.far
     x, c, z = me.x, me.c, me.z
@@ -260,7 +303,7 @@
 
 
 def reduce_part(me, sems, view, bufs, emit, credit, wait_credit, give_credit):
-    rc, ry, rx, rz, fin, far = [functools.partial(slot, ref, i) for ref, i in bufs]
+    rc, ry, rx, rz, fin, far = bufs
     (a, b), (ta, tb) = me.own, me.far
     x, c, z = me.x, me.c, me.z
     xo = me.x_far
@@ -468,15 +511,19 @@
     return jnp.sum(values, axis=0, keepdims=True)
 
 
+def cut(sizes):
+    return [pl.ds(128 * sum(sizes[:i]), 128 * size) for i, size in enumerate(sizes)]
+
+
 def layer_kernel(
-    depth, lanes, halves,
+    depth, lanes,
     x_h, cot_h, seg, live, expert, g1, b1, qb, vb, ob, g2, b2, ib, yb,
     q_w, k_w, v_w, o_w, w_in, w_out,
     out_h, dx_h, counts, d_q, d_k, d_v, d_o, d_in, d_out,
     d_g1, d_b1, d_qb, d_vb, d_ob, d_g2, d_b2, d_ib, d_yb,
-    qkv_h, a_h, pb_h, z_h, h_h,
+    qkv_h, a_h, pb_h, z_h, h_h, go_h,
     ga, gi, go, s1, s2, pa, po, x_s, o_s, c_s, xh, dattn, hd, tok, rstd_s,
-    rc, ry, rx, rz, fin, far, vec, vec_pair, vec_stack, cnt, cnt_pair, cnt_stack, ib_s,
+    rc, ry, rx, rz, fin, far, vec, vec_pair, vec_stack, cnt, cnt_pair, cnt_stack, ib_s, yb_s,
     local, send, recv, rsend, rrecv, csend, crecv, vsend, vrecv, credit,
 ):
     me = Place(depth, lanes)
@@ -485,10 +532,12 @@
     row_total, slots = seg.shape
     blocks = s1.shape[0]
     x_, c_, z_ = me.x, me.c, me.z
-    part = width // halves
-    pairs_half = part // 128
     per = depth // 4
-    part_total = 3 * halves
+    gathered, reduced = [[cut(sizes) for sizes in cuts] for cuts in (GATHER_CUTS, REDUCE_CUTS)]
+    count_part = sum(len(cuts) for cuts in gathered)
+    reduce_base = count_part + 1
+    reduce_total = sum(len(cuts) for cuts in reduced)
+    vec_part = reduce_base + reduce_total
     used = [2]
 
     def move(src, dst):
@@ -522,11 +571,9 @@
     for m in filled:
         m.wait()
 
-    def view_of(g, h, first, second, third):
-        cols = pl.ds(h * part, part)
-
+    def view_of(g, cols, first, second, third):
         def view(u, zs, xs, cs):
-            if g == 2:
+            if g > 1:
                 return third.at[zs, xs, cs, u, :, cols]
             return (first, second)[g].at[u, zs, xs, cs, :, cols]
 
@@ -534,19 +581,23 @@
 
     flow, gather_sems, reduce_sems = Flow(TABLE), [], []
     for g in range(3):
-        for h in range(halves):
-            sems = Sems(send, recv, g * halves + h)
+        for cols_g in gathered[g]:
+            sems = Sems(send, recv, len(gather_sems))
+            flow.begin(len(gather_sems), gather_part(me, sems, view_of(g, cols_g, ga, gi, go)))
             gather_sems.append(sems)
-            flow.begin(g * halves + h, gather_part(me, sems, view_of(g, h, ga, gi, go)))
     flow.pump()
     m_cot = move(cot_h, dattn)
     vec[...] = jnp.zeros_like(vec)
     for u in range(blocks):
         ib_s[u : u + 1, :] = ib[:, pl.ds(u * width, width)]
-
-    def ready(i):
+    yb_s[0:1, :] = yb[...]
+
+    arrived = [0]
+
+    def ready():
         flow.pump()
-        flow.finish(i)
+        flow.finish(arrived[0])
+        arrived[0] += 1
 
     cnt[...] = jnp.zeros_like(cnt)
     for r in range(row_total):
@@ -568,7 +619,7 @@
             rows = pl.ds(r * slots, slots)
             tok[rows, :] = tok[rows, :] * scale
 
-    flow.begin(part_total, all_sum(me, csems, cnt, cnt_pair, cnt_stack, count_out))
+    flow.begin(count_part, all_sum(me, csems, cnt, cnt_pair, cnt_stack, count_out))
     flow.pump()
     m_x.wait()
 
@@ -594,25 +645,24 @@
         flow.pump()
 
     masks = lane_halves()
-    for h in range(halves):
-        cols_h = pl.ds(h * part, part)
-        ready(h)
-
-        def project(r):
+    for cols_h in gathered[0]:
+        ready()
+
+        def project(r, cols_h=cols_h):
             rows = row(r)
             a_row = s1[3, rows, :]
             for u, add in enumerate((qb, None, vb)):
-                value = dot_nn(a_row, ga[u, :, :, :, :, cols_h].reshape(width, part))
+                value = dot_nn(a_row, ga[u, :, :, :, :, cols_h].reshape(width, cols_h.size))
                 if add is not None:
                     value = value + add[:, cols_h]
                 s1[u, rows, cols_h] = value.astype(BF)
 
         stepped(flow, row_total, project)
 
-        def attend(r):
+        def attend(r, cols_h=cols_h):
             rows = row(r)
-            for p in range(pairs_half):
-                cols = pl.ds(h * part + p * 128, 128)
+            for start in range(cols_h.start, cols_h.start + cols_h.size, 128):
+                cols = pl.ds(start, 128)
                 q2, k2, v2 = s1[0, rows, cols], s1[1, rows, cols], s1[2, rows, cols]
                 mixed = jnp.zeros((slots, 128), F32)
                 for i in range(2):
@@ -621,7 +671,7 @@
                     terms = jnp.exp(scores - top)
                     inv = 1.0 / jnp.sum(terms, axis=-1, keepdims=True)
                     probs = (terms * inv).astype(BF)
-                    head = (h * pairs_half + p) * 2 + i
+                    head = start // 64 + i
                     s2[head // 3, rows, pl.ds((head % 3) * slots, slots)] = probs
                     mixed = mixed + dot_nn(probs, v2 * masks[i])
                 o_s[rows, cols] = mixed.astype(BF)
@@ -645,13 +695,12 @@
     for m in (m_a, *m_qkv, m_pb):
         m.wait()
     pair_rows = row_total // 2
-    for h in range(halves):
-        cols_h = pl.ds(h * part, part)
-        ready(halves + h)
-
-        def hidden(t):
+    for cols_h in gathered[1]:
+        ready()
+
+        def hidden(t, cols_h=cols_h):
             u, first = t // pair_rows, 2 * lax.rem(t, pair_rows)
-            weight = gi[u, :, :, :, :, cols_h].reshape(width, part)
+            weight = gi[u, :, :, :, :, cols_h].reshape(width, cols_h.size)
             for s in range(2):
                 rows = row(first + s)
                 pre = dot_nn(c_s[rows, :], weight) + ib_s[pl.ds(u, 1), cols_h]
@@ -661,11 +710,12 @@
 
         stepped(flow, blocks * pair_rows, hidden)
     m_z = move(s1, z_h)
-    flow.finish(part_total)
+    flow.finish(count_part)
     m_cot.wait()
 
-    def begin(g, h, i):
-        cols = pl.ds(h * part, part)
+    def begin(g, cols):
+        i = len(reduce_sems)
+        at = pl.ds((2 - g) * width + cols.start, cols.size)
 
         def emit(u, mine, k, value):
             value = value.astype(F32)
@@ -680,19 +730,20 @@
                 def _():
                     (d_v, d_o)[k][:, cols] = value
             elif g == 1:
-                d_in[:, pl.ds(pl.multiple_of(u * width + h * part, 128), part)] = value
+                d_in[:, pl.ds(pl.multiple_of(u * width + cols.start, 128), cols.size)] = value
             else:
                 d_out[pl.ds(pl.multiple_of(u * rows_w, 8), rows_w), cols] = value
 
         sems = Sems(rsend, rrecv, i)
         reduce_sems.append(sems)
-        bufs = [(rc, i % 2)] + [(t, i) for t in (ry, rx, rz, fin, far)]
-        base = part_total + 1
-        while i >= 2 and flow.count[base + i - 2] < 4:
-            flow.step(base + i - 2)
-        view = view_of(g, h, pa, gi, po)
-        flow.begin(base + i, reduce_part(me, sems, view, bufs, emit, credit, i >= 2, i < part_total - 2))
-        flow.step(base + i)
+        bufs = [functools.partial(strip, rc, pl.ds(0, cols.size), i % 2)]
+        bufs += [functools.partial(strip, t, at) for t in (ry, rx, rz, fin, far)]
+        while i >= 2 and flow.count[reduce_base + i - 2] < 4:
+            flow.step(reduce_base + i - 2)
+        view = view_of(g, cols, pa, None, po) if g != 1 else view_of(2, cols, None, None, go)
+        give = i < reduce_total - 2
+        flow.begin(reduce_base + i, reduce_part(me, sems, view, bufs, emit, credit, i >= 2, give))
+        flow.step(reduce_base + i)
 
     def scaled(r):
         rows = row(r)
@@ -701,19 +752,18 @@
         vec[7:8, :] += down_sum(value.astype(F32))
 
     stepped(flow, row_total, scaled)
-    for h in range(halves):
-        cols_h = pl.ds(h * part, part)
-
-        def out_grad(u):
+    for cols_h in reduced[0]:
+        def out_grad(u, cols_h=cols_h):
             value = dot_tn(s1[u], gb[:, cols_h]).astype(BF)
-            po[pl.ds(u * per, per), :, :, :, :, cols_h] = value.reshape(per, 2, 2, 4, rows_w, part)
+            po[pl.ds(u * per, per), :, :, :, :, cols_h] = value.reshape(per, 2, 2, 4, rows_w, cols_h.size)
 
         stepped(flow, blocks, out_grad)
-        begin(2, h, h)
+        begin(2, cols_h)
     m_z.wait()
     m_q = [move(qkv_h.at[u], s1.at[u]) for u in range(3)] + [move(a_h, s1.at[3])]
-    for h in range(halves):
-        ready(2 * halves + h)
+    for _ in gathered[2]:
+        ready()
+    m_go = move(go, go_h)
 
     def hidden_grad(t):
         u, rows = t // row_total, row(lax.rem(t, row_total))
@@ -723,6 +773,17 @@
         vec[pl.ds(8 + u, 1), :] += down_sum(value.astype(F32))
 
     stepped(flow, blocks * row_total, hidden_grad)
+    for s in gather_sems:
+        s.drain()
+    csems.drain()
+    m_go.wait()
+    for cols_h in reduced[1]:
+        def in_grad(u, cols_h=cols_h):
+            value = dot_tn(c_s[...], s2[u, :, cols_h]).astype(BF)
+            go[:, :, :, u, :, cols_h] = value.reshape(depth, 2, 2, rows_w, cols_h.size)
+
+        stepped(flow, blocks, in_grad)
+        begin(1, cols_h)
     m_h.wait()
 
     def mid_grad(r):
@@ -741,23 +802,10 @@
         vec[4:5, :] += down_sum(value.astype(F32))
 
     stepped(flow, row_total, mid_grad)
-    for s in gather_sems:
-        s.drain()
-    csems.drain()
-    for h in range(halves):
-        cols_h = pl.ds(h * part, part)
-
-        def in_grad(u):
-            value = dot_tn(c_s[...], s2[u, :, cols_h]).astype(BF)
-            gi[u, :, :, :, :, cols_h] = value.reshape(depth, 2, 2, rows_w, part)
-
-        stepped(flow, blocks, in_grad)
-        begin(1, h, halves + h)
     m_p = move(pb_h, s2)
-    for h in range(halves):
-        cols_h = pl.ds(h * part, part)
+    for cols_h in reduced[2]:
         value = dot_tn(o_s[...], dattn[:, cols_h]).astype(BF)
-        pa[3, :, :, :, :, cols_h] = value.reshape(depth, 2, 2, rows_w, part)
+        pa[3, :, :, :, :, cols_h] = value.reshape(depth, 2, 2, rows_w, cols_h.size)
         flow.pump()
 
     def mixed_grad(r):
@@ -768,23 +816,22 @@
     for m in m_q:
         m.wait()
     m_p.wait()
-    for h in range(halves):
-        cols_h = pl.ds(h * part, part)
-
-        def attend_back(r):
+    for cols_h in reduced[2]:
+        def attend_back(r, cols_h=cols_h):
             rows = row(r)
-            for p in range(pairs_half):
-                cols = pl.ds(h * part + p * 128, 128)
+            for start in range(cols_h.start, cols_h.start + cols_h.size, 128):
+                cols = pl.ds(start, 128)
                 q2, k2, v2, do2 = s1[0, rows, cols], s1[1, rows, cols], s1[2, rows, cols], gb[rows, cols]
                 dq = jnp.zeros((slots, 128), F32)
                 dk, dv = dq, dq
+                both = do2.astype(F32) * o_s[rows, cols].astype(F32)
                 for i in range(2):
-                    head = (h * pairs_half + p) * 2 + i
+                    head = start // 64 + i
                     probs = s2[head // 3, rows, pl.ds((head % 3) * slots, slots)]
                     do1 = do2 * masks[i]
                     dp = dot_nt(do1, v2)
                     wide = probs.astype(F32)
-                    inner = jnp.sum(dp * wide, axis=-1, keepdims=True)
+                    inner = jnp.sum(both * masks[i].astype(F32), axis=-1, keepdims=True)
                     ds = (wide * (dp - inner)).astype(BF)
                     dq = dq + dot_nn(ds, k2 * masks[i])
                     dk = dk + dot_tn(ds, q2 * masks[i])
@@ -797,16 +844,21 @@
                 vec[3:4, cols] += down_sum(dv.astype(F32))
 
         stepped(flow, row_total, attend_back)
-        if h == halves - 1:
+        if cols_h is reduced[2][-1]:
             m_x = move(x_h, x_s)
 
-        def project_grad(u):
+        def project_grad(u, cols_h=cols_h):
             value = dot_tn(s1[3], s1[u, :, cols_h]).astype(BF)
-            pa[u, :, :, :, :, cols_h] = value.reshape(depth, 2, 2, rows_w, part)
+            pa[u, :, :, :, :, cols_h] = value.reshape(depth, 2, 2, rows_w, cols_h.size)
 
         stepped(flow, 3, project_grad)
-        begin(0, h, 2 * halves + h)
+        begin(0, cols_h)
     m_z = move(z_h, s2)
+    for i, sems in enumerate(reduce_sems):
+        if len(reduced[0]) <= i < len(reduced[0]) + len(reduced[1]):
+            flow.finish(reduce_base + i)
+            sems.drain()
+    m_go = move(go_h, go)
     m_x.wait()
 
     def last_grad(r):
@@ -831,20 +883,22 @@
         for u in range(blocks):
             d_ib[pl.ds(u * width, width)] = total[8 + u]
 
-    vec_part = 2 * part_total + 1
     flow.begin(vec_part, all_sum(me, vsems, vec, vec_pair, vec_stack, vec_out))
     flow.step(vec_part)
     m_z.wait()
     m_h.wait()
-
-    def outward(r):
-        rows = row(r)
-        value = hd[rows, :] + yb[...]
+    m_go.wait()
+
+    half = width // 2
+
+    def outward(t):
+        rows, cols = row(t // 2), pl.ds(pl.multiple_of(lax.rem(t, 2) * half, half), half)
+        value = hd[rows, cols] + yb_s[0:1, cols]
         for u in range(blocks):
-            value = value + dot_nn(s2[u, rows, :], go[u * per : (u + 1) * per].reshape(width, width))
-        gb[rows, :] = value.astype(BF)
-
-    stepped(flow, row_total, outward)
+            value = value + dot_nn(s2[u, rows, :], go[u * per : (u + 1) * per, :, :, :, :, cols].reshape(width, half))
+        gb[rows, cols] = value.astype(BF)
+
+    stepped(flow, 2 * row_total, outward)
     m_out = move(gb, out_h)
     flow.pump()
     flow.finish_all()
@@ -855,13 +909,14 @@
     m_out.wait()
 
 
-def whole_layer(depth, lanes, halves, x, cot, seg, live, expert, vectors, weights):
+def whole_layer(depth, lanes, x, cot, seg, live, expert, vectors, weights):
     tokens, width = x.shape
     row_total, slots = seg.shape
     rows_w = weights[0].shape[0]
     ff = weights[4].shape[1]
     blocks = ff // width
-    parts, cols = 3 * halves, width // halves
+    g_parts, r_parts = [sum(len(sizes) for sizes in cuts) for cuts in (GATHER_CUTS, REDUCE_CUTS)]
+    cols = 128 * max(max(sizes) for sizes in REDUCE_CUTS)
     g_per, r_per = gather_copies(depth), reduce_copies(depth, lanes)
     bits = max(lanes.bit_length() - 1, 1)
     pair_n, pair_c, _ = all_sum_sizes(depth, lanes)
@@ -878,21 +933,21 @@
     n = lambda *s: pltpu.VMEM(s, jnp.int32)
     dma = lambda *s: pltpu.SemaphoreType.DMA(s)
     return pl.pallas_call(
-        functools.partial(layer_kernel, depth, lanes, halves),
+        functools.partial(layer_kernel, depth, lanes),
         out_shape=[like(flat, BF), like(flat, BF), like((3,), jnp.int32)]
         + [o(rows_w, width)] * 4 + [o(rows_w, ff), o(4 * rows_w, width)]
         + [o(width)] * 7 + [o(ff), o(width)]
-        + [like((3, *flat), BF), like(flat, BF), like(wide, BF), like(wide, BF), like(flat, F32)],
+        + [like((3, *flat), BF), like(flat, BF), like(wide, BF), like(wide, BF), like(flat, F32), like(unit_o, BF)],
         in_specs=[anyspec] * 2 + [vspec] * 2 + [sspec] + [vspec] * 9 + [anyspec] * 6,
-        out_specs=[anyspec] * 2 + [sspec] + [vspec] * 15 + [anyspec] * 5,
+        out_specs=[anyspec] * 2 + [sspec] + [vspec] * 15 + [anyspec] * 6,
         scratch_shapes=[
             v(*unit), v(*unit), v(*unit_o), v(*wide), v(*wide), v(*unit), v(*unit_o),
             v(*flat), v(*flat), v(*flat), v(*flat), v(*flat), f(*flat), f(tokens, 128), f(tokens, 128),
-            v(2, 4, depth, 2, rows_w, cols), v(parts, 3, depth, rows_w, cols), v(parts, 3, depth, rows_w, cols),
-            v(parts, 2, depth - 1, rows_w, cols), v(parts, bits, 2, rows_w, cols), v(parts, bits, 2, rows_w, cols),
+            v(2, 4, depth, 2, rows_w, cols), v(3, depth, rows_w, 3 * width), v(3, depth, rows_w, 3 * width),
+            v(2, depth - 1, rows_w, 3 * width), v(bits, 2, rows_w, 3 * width), v(bits, 2, rows_w, 3 * width),
             f(vec_rows, width), f(pair_n, vec_rows, width), f(depth, vec_rows, width),
-            n(8, slots), n(pair_n, 8, slots), n(depth, 8, slots), f(-(-blocks // 8) * 8, width),
-            dma(40), dma(parts, g_per), dma(parts, g_per), dma(parts, r_per), dma(parts, r_per),
+            n(8, slots), n(pair_n, 8, slots), n(depth, 8, slots), f(-(-blocks // 8) * 8, width), f(8, width),
+            dma(40), dma(g_parts, g_per), dma(g_parts, g_per), dma(r_parts, r_per), dma(r_parts, r_per),
             dma(1, pair_c), dma(1, pair_c), dma(1, pair_c), dma(1, pair_c), pltpu.SemaphoreType.REGULAR,
         ],
         compiler_params=pltpu.CompilerParams(collective_id=0, has_side_effects=True, vmem_limit_bytes=VMEM_BYTES),
@@ -943,7 +998,7 @@
     vectors = [norm1_gain, norm1_bias, q_bias, v_bias, o_bias, norm2_gain, norm2_bias, in_bias, out_bias]
     weights = (q_weight, k_weight, v_weight, o_weight, in_weight, out_weight)
     layer_out, input_grad, counts, *grads = whole_layer(
-        depth, lanes, HALVES, x, cotangent.reshape(tokens, width_all), segment_ids, live_mask, expert_ids, vectors, weights
+        depth, lanes, x, cotangent.reshape(tokens, width_all), segment_ids, live_mask, expert_ids, vectors, weights
     )
     (
         layer_out, input_grad, d_q, d_k, d_v, d_o, d_in, d_out,

time: 179 us -> 174 us (0.972)
  Pallas kernels: 178 us -> 173 us
    pallas_call x1, Pallas kernels: 173 us -> 168 us  [whole_layer(): pl.pallas_call(functools.partial(layer_kernel, depth, lanes), out_shape=[...]
where the time goes in v3:
time: 174 us
  Pallas kernels  173 us (99%)
    pallas_call x1, Pallas kernels, whole_layer(): pl.pallas_call(functools.partial(layer_kernel, depth, lanes), out_shape=[...  168 us
    pallas_call x1, Pallas kernels, hand_over(): pl.pallas_call(functools.partial(hand_over_kernel, count), out_shape=[jax...  5.2 us

profile of v3, /device:TPU:0, one launch (start us, length us, event | category | flops | bytes accessed | tf_op | source)
XLA Modules:
  0.0 173.7 jit_solution(9241997078762835365)
XLA Ops:
  0.7 167.6 %whole_layer.1 = (bf16[1024,768]{1,0:T(8,128)(2,1)}, bf16[1024,768]{1,0:T(8,128)(2,1)}, s32[3]{0:T(128)}, f32[48,768]{1,0:T(8,128)}, f32[48,768]{1,0:T(8,128)}, ...) custom-call(bf16[1024,768]{1,0:T(8,128)(2,1)} %bitcast.4, ...), custom_call_target="tpu_custom_call" | custom-call | tf_op jit(solution)/shard_map/whole_layer/pallas_call | solution.py:935
  168.3 5.2 %hand_over.1 = (bf16[1024,768]{1,0:T(8,128)(2,1)}, bf16[1024,768]{1,0:T(8,128)(2,1)}, f32[48,768]{1,0:T(8,128)}, f32[48,768]{1,0:T(8,128)}, f32[48,768]{1,0:T(8,...) custom-call(bf16[1024,768]{1,0:T(8,128)(2,1)} %get-tuple-element.54., ...), custom_call_target="tpu_custom_call" | custom-call | tf_op jit(solution)/shard_map/hand_over/pallas_call | solution.py:978

commit v4 on v3

--- a/solution.py
+++ b/solution.py
@@ -18,62 +18,63 @@
     (8,),
     (),
     (),
+    (),
     (8,),
     (),
     (),
     (),
-    (8,),
-    (),
-    (0, 1, 1, 0, 8, 0, 0, 0, 1, 2, 2, 1, 0, 2, 3, 3, 2, 0, 0),
-    (1, 1, 1),
-    (),
-    (),
-    (),
-    (),
-    (3, 4, 4),
-    (2, 2, 2),
-    (),
-    (3, 1, 1, 1),
-    (),
-    (),
-    (4, 5, 5),
-    (),
+    (),
+    (8, 0, 1, 1, 0, 8, 0, 0, 0, 1, 2, 2, 1, 0, 2, 3, 3, 0, 2, 1, 1, 1, 0),
+    (),
+    (),
+    (),
+    (),
+    (),
+    (3, 4),
+    (2, 4),
+    (1, 2, 1, 2),
+    (3, 1),
     (3,),
-    (2, 2),
-    (3, 4, 3),
-    (2,),
-    (),
+    (),
+    (),
+    (4, 5),
+    (2, 5),
+    (2, 3, 3),
     (4,),
+    (4, 3, 2),
     (),
     (),
     (),
     (5, 6),
+    (),
     (3, 6),
-    (3, 5),
     (4, 4),
     (3, 5),
+    (4, 5),
+    (),
+    (6, 7),
     (4,),
-    (),
-    (6, 7),
-    (),
-    (),
-    (4, 7),
-    (5, 5),
+    (7, 5, 5),
+    (),
+    (),
     (),
     (4,),
-    (),
-    (5, 6),
-    (),
-    (),
-    (),
-    (),
-    (),
-    (),
-    (),
-    (),
-    (),
+    (6,),
+    (5,),
+    (),
+    (),
+    (),
+    (),
+    (6,),
+    (),
+    (),
+    (),
+    (),
+    (5,),
     (7,),
-    (5, 6, 7, 6, 5),
+    (),
+    (7, 5),
+    (6, 6),
     (),
     (),
     (),
@@ -88,91 +89,90 @@
     (),
     (),
     (),
-    (),
-    (),
-    (6, 7, 7),
-    (),
-    (6, 7),
+    (7, 7),
+    (7,),
+    (6,),
+    (),
+    (),
+    (9, 9, 6),
+    (7, 7, 9, 7),
+    (),
+    (10, 10),
+    (),
+    (),
+    (),
+    (),
     (9, 9),
-    (9, 6),
-    (7, 7, 10, 10, 10, 7),
-    (),
-    (),
-    (),
-    (),
-    (),
-    (),
-    (),
-    (),
-    (),
-    (),
+    (),
+    (),
+    (),
+    (),
+    (),
+    (10,),
+    (),
+    (),
+    (),
+    (10, 10),
     (),
     (9, 9),
     (),
     (),
     (),
-    (),
-    (),
-    (10, 10),
-    (),
-    (),
+    (10,),
+    (11, 11),
+    (10, 11),
     (9, 9),
+    (10, 11),
+    (10, 11),
+    (9, 9),
+    (),
+    (10,),
+    (12, 12),
+    (),
+    (11, 10),
+    (),
+    (),
+    (12,),
+    (11,),
+    (),
+    (11, 12, 12),
+    (),
+    (),
     (),
     (11, 11),
     (),
-    (10, 11),
-    (10, 11, 12),
-    (9, 9),
-    (12, 11),
-    (),
-    (),
-    (),
-    (9, 9, 10, 11, 10),
-    (),
-    (),
-    (),
-    (12,),
-    (),
-    (10, 12, 10),
-    (12,),
-    (),
-    (11, 11),
-    (),
-    (),
-    (12,),
-    (13, 13, 13),
-    (11, 12, 11),
-    (),
-    (),
-    (12,),
-    (),
-    (11,),
-    (),
     (12, 13, 13),
+    (11, 12, 13),
+    (),
+    (),
+    (),
+    (),
+    (13, 13),
+    (),
+    (),
     (12,),
     (14, 14),
     (),
-    (),
-    (),
-    (14, 12),
-    (),
-    (),
+    (12,),
+    (),
+    (13, 14),
     (13,),
+    (12,),
     (15, 15),
     (),
+    (14, 14),
+    (13, 15),
     (13, 15, 16, 16),
-    (13, 14, 14),
-    (15,),
-    (13, 15),
-    (13, 16, 17, 16),
     (14, 15, 16),
-    (),
     (13, 14),
-    (15,),
-    (15, 16, 17),
-    (16,),
-    (),
-    (14, 17, 15, 15, 16, 14, 14, 15, 16, 16, 16, 14, 17),
+    (13, 17),
+    (15, 16, 16),
+    (),
+    (14, 15),
+    (17,),
+    (14, 15, 16, 16),
+    (14,),
+    (15, 17, 15, 14, 15, 16, 16, 16, 16, 17),
 )
 
 MESH = pl.DeviceIdType.MESH
@@ -524,7 +524,7 @@
     qkv_h, a_h, pb_h, z_h, h_h, go_h,
     ga, gi, go, s1, s2, pa, po, x_s, o_s, c_s, xh, dattn, hd, tok, rstd_s,
     rc, ry, rx, rz, fin, far, vec, vec_pair, vec_stack, cnt, cnt_pair, cnt_stack, ib_s, yb_s,
-    local, send, recv, rsend, rrecv, csend, crecv, vsend, vrecv, credit,
+    local, by_row, send, recv, rsend, rrecv, csend, crecv, vsend, vrecv, credit,
 ):
     me = Place(depth, lanes)
     g1, b1, qb, vb, ob, g2, b2, ib, yb = [Row(t) for t in (g1, b1, qb, vb, ob, g2, b2, ib, yb)]
@@ -629,7 +629,7 @@
         s1[3, rows, :] = (centred * rstd * g1[...] + b1[...]).astype(BF)
 
     stepped(flow, row_total, first_norm)
-    m_a = move(s1.at[3], a_h)
+    spilled = [move(s1.at[3], a_h)]
 
     row_pos = lax.broadcasted_iota(jnp.int32, (slots, slots), 0)
     col_pos = lax.broadcasted_iota(jnp.int32, (slots, slots), 1)
@@ -677,8 +677,11 @@
                 o_s[rows, cols] = mixed.astype(BF)
 
         stepped(flow, row_total, attend)
-    m_qkv = [move(s1.at[u], qkv_h.at[u]) for u in range(3)]
-    m_pb = move(s2, pb_h)
+        for u in range(3):
+            spilled.append(move(s1.at[u, :, cols_h], qkv_h.at[u, :, cols_h]))
+        for head in range(cols_h.start // 64, (cols_h.start + cols_h.size) // 64):
+            cols = pl.ds((head % 3) * slots, slots)
+            spilled.append(move(s2.at[head // 3, :, cols], pb_h.at[head // 3, :, cols]))
 
     def second_norm(r):
         rows = row(r)
@@ -692,7 +695,7 @@
 
     stepped(flow, row_total, second_norm)
     m_h = move(hd, h_h)
-    for m in (m_a, *m_qkv, m_pb):
+    for m in spilled:
         m.wait()
     pair_rows = row_total // 2
     for cols_h in gathered[1]:
@@ -861,6 +864,12 @@
     m_go = move(go_h, go)
     m_x.wait()
 
+    def h_back(r):
+        return pltpu.make_async_copy(h_h.at[row(r), :], hd.at[row(r), :], by_row.at[0, r])
+
+    def dx_back(r):
+        return pltpu.make_async_copy(dattn.at[row(r), :], dx_h.at[row(r), :], by_row.at[1, r])
+
     def last_grad(r):
         rows = row(r)
         grad = dot_nt(s1[0, rows, :], ga[0].reshape(width, width))
@@ -871,10 +880,10 @@
         vec[0:1, :] += down_sum(grad * normed)
         vec[1:2, :] += down_sum(grad)
         dattn[rows, :] = (hd[rows, :] + norm_back(grad * g1[...], normed, rstd)).astype(BF)
+        dx_back(r).start()
+        h_back(r).start()
 
     stepped(flow, row_total, last_grad)
-    m_h = move(h_h, hd)
-    m_dx = move(dattn, dx_h)
     vsems = Sems(vsend, vrecv, 0)
 
     def vec_out(total):
@@ -886,8 +895,10 @@
     flow.begin(vec_part, all_sum(me, vsems, vec, vec_pair, vec_stack, vec_out))
     flow.step(vec_part)
     m_z.wait()
-    m_h.wait()
     m_go.wait()
+    for r in range(row_total):
+        h_back(r).wait()
+        dx_back(r).wait()
 
     half = width // 2
 
@@ -905,7 +916,6 @@
     for s in reduce_sems:
         s.drain()
     vsems.drain()
-    m_dx.wait()
     m_out.wait()
 
 
@@ -947,7 +957,7 @@
             v(2, depth - 1, rows_w, 3 * width), v(bits, 2, rows_w, 3 * width), v(bits, 2, rows_w, 3 * width),
             f(vec_rows, width), f(pair_n, vec_rows, width), f(depth, vec_rows, width),
             n(8, slots), n(pair_n, 8, slots), n(depth, 8, slots), f(-(-blocks // 8) * 8, width), f(8, width),
-            dma(40), dma(g_parts, g_per), dma(g_parts, g_per), dma(r_parts, r_per), dma(r_parts, r_per),
+            dma(64), dma(2, row_total), dma(g_parts, g_per), dma(g_parts, g_per), dma(r_parts, r_per), dma(r_parts, r_per),
             dma(1, pair_c), dma(1, pair_c), dma(1, pair_c), dma(1, pair_c), pltpu.SemaphoreType.REGULAR,
         ],
         compiler_params=pltpu.CompilerParams(collective_id=0, has_side_effects=True, vmem_limit_bytes=VMEM_BYTES),

time: 174 us -> 171 us (0.983)
  Pallas kernels: 173 us -> 169 us
    pallas_call x1, Pallas kernels: 168 us -> 164 us  [whole_layer(): pl.pallas_call(functools.partial(layer_kernel, depth, lanes), out_shape=[...]
where the time goes in v4:
time: 171 us; the launch traced here: 170 us
  Pallas kernels  169 us (99%)
    pallas_call x1, Pallas kernels, whole_layer(): pl.pallas_call(functools.partial(layer_kernel, depth, lanes), out_shape=[...  164 us
    pallas_call x1, Pallas kernels, hand_over(): pl.pallas_call(functools.partial(hand_over_kernel, count), out_shape=[jax...  5.2 us

profile of v4, /device:TPU:0, one launch (start us, length us, event | category | flops | bytes accessed | tf_op | source)
XLA Modules:
  0.0 170.3 jit_solution(14252420511068202162)
XLA Ops:
  0.7 164.3 %whole_layer.1 = (bf16[1024,768]{1,0:T(8,128)(2,1)}, bf16[1024,768]{1,0:T(8,128)(2,1)}, s32[3]{0:T(128)}, f32[48,768]{1,0:T(8,128)}, f32[48,768]{1,0:T(8,128)}, ...) custom-call(bf16[1024,768]{1,0:T(8,128)(2,1)} %bitcast.4, ...), custom_call_target="tpu_custom_call" | custom-call | tf_op jit(solution)/shard_map/whole_layer/pallas_call | solution.py:945
  164.9 5.2 %hand_over.1 = (bf16[1024,768]{1,0:T(8,128)(2,1)}, bf16[1024,768]{1,0:T(8,128)(2,1)}, f32[48,768]{1,0:T(8,128)}, f32[48,768]{1,0:T(8,128)}, f32[48,768]{1,0:T(8,...) custom-call(bf16[1024,768]{1,0:T(8,128)(2,1)} %get-tuple-element.54., ...), custom_call_target="tpu_custom_call" | custom-call | tf_op jit(solution)/shard_map/hand_over/pallas_call | solution.py:988

commit v5 on v4

--- a/solution.py
+++ b/solution.py
@@ -1,4 +1,5 @@
 import functools
+import math
 
 import jax
 import jax.numpy as jnp
@@ -974,9 +975,9 @@
         m.start()
     for i in range(3):
         refs[2 * count + 1][i] = refs[count][i]
-    for first, second in zip(into, out):
-        first.wait()
-        second.start()
+    for i in sorted(range(count), key=lambda i: math.prod(sources[i].shape)):
+        into[i].wait()
+        out[i].start()
     for m in out:
         m.wait()
 

time: 171 us -> 171 us (level)
  no operation moved by 1% of the time
where the time goes in v5:
time: 171 us
  Pallas kernels  170 us (99%)
    pallas_call x1, Pallas kernels, whole_layer(): pl.pallas_call(functools.partial(layer_kernel, depth, lanes), out_shape=[...  164 us
    pallas_call x1, Pallas kernels, hand_over(): pl.pallas_call(functools.partial(hand_over_kernel, count), out_shape=[jax...  6.02 us

profile of v5, /device:TPU:0, one launch (start us, length us, event | category | flops | bytes accessed | tf_op | source)
XLA Modules:
  0.0 171.1 jit_solution(3303393203610925141)
XLA Ops:
  0.7 164.3 %whole_layer.1 = (bf16[1024,768]{1,0:T(8,128)(2,1)}, bf16[1024,768]{1,0:T(8,128)(2,1)}, s32[3]{0:T(128)}, f32[48,768]{1,0:T(8,128)}, f32[48,768]{1,0:T(8,128)}, ...) custom-call(bf16[1024,768]{1,0:T(8,128)(2,1)} %bitcast.4, ...), custom_call_target="tpu_custom_call" | custom-call | tf_op jit(solution)/shard_map/whole_layer/pallas_call | solution.py:946
  164.9 6.0 %hand_over.1 = (bf16[1024,768]{1,0:T(8,128)(2,1)}, bf16[1024,768]{1,0:T(8,128)(2,1)}, f32[48,768]{1,0:T(8,128)}, f32[48,768]{1,0:T(8,128)}, f32[48,768]{1,0:T(8,...) custom-call(bf16[1024,768]{1,0:T(8,128)(2,1)} %get-tuple-element.54., ...), custom_call_target="tpu_custom_call" | custom-call | tf_op jit(solution)/shard_map/hand_over/pallas_call | solution.py:989
